TPU v7x, 256 devices: a whole 4x4x8 slice. The times are simulated.
256 devices in a mesh: head: 8 (over y, core), ctx: 32 (over x, z).
Axes of the slice: x: 4, y: 4, z: 8, core: 2. Of those that a mesh axis runs over, the one named last changes fastest.
Arguments:
- main_queries: bfloat16 [512, 128, 192], P(None, 'head'), may hold values from -6 to 6
- main_keys: bfloat16 [32768, 128, 192], P('ctx', 'head'), may hold values from -7 to 7
- log_sums: float32 [512, 128], P(None, 'head'), may hold values from 10 to 13
- index_queries: bfloat16 [512, 64, 128], P('head'), may hold values from -2 to 2
- index_weights: bfloat16 [512, 64], P('head'), may hold values from -3 to 3
- index_keys: bfloat16 [32768, 128], P('ctx'), may hold values from -7 to 7
- loss_weights: float32 [512], P('head'), may hold values from 4 to 64
Outputs:
- query_grad: bfloat16 [512, 64, 128], P('head', 'ctx')
- weight_grad: float32 [512, 64], P('head', 'ctx')
- key_grad: bfloat16 [32768, 128], P('ctx', 'head')
All inputs are finite; a program needn't handle non-finite values.
Results may differ from a plain program's by a relative error of at most 0.023.
Values may be sent and summed in bfloat16 or wider, within the bound.
No kernel may reach another device: no remote copies, remote signals or barrier semaphores. Data moves between devices by JAX's collectives and lax.ppermute only.
A program may use at most 128 MiB of HBM per device.

v0:
```python
import jax
import jax.numpy as jnp
from jax import lax
from jax.sharding import PartitionSpec as P

IH = 64
ID = 128


def split_up(array, dim, length):
    lengths = array.shape
    pieces = array.reshape(*lengths[:dim], length, lengths[dim] // length, *lengths[dim + 1 :])
    return jnp.moveaxis(pieces, dim, 0)


def summed_on_arrival(array, axis, dim):
    pieces = split_up(array, dim, lax.axis_size(axis))
    arrived = lax.all_to_all(pieces, axis, split_axis=0, concat_axis=0, tiled=True)
    return arrived.astype(jnp.float32).sum(axis=0)


def from_everyone(array, axis):
    copies = jnp.broadcast_to(array, (lax.axis_size(axis), *array.shape))
    return lax.all_to_all(copies, axis, split_axis=0, concat_axis=0, tiled=True)


def gathered_once(array, axis):
    leaves = jax.tree.leaves(array)
    order = sorted(range(len(leaves)), key=lambda k: -leaves[k].size)
    width = (1, *leaves[order[0]].shape)[-1]
    lines = [
        jnp.pad(leaves[k].reshape(-1), (0, -leaves[k].size % width)).reshape(-1, width)
        for k in order
    ]
    both, at, found = (from_everyone(jnp.concatenate(lines), axis), 0, {})
    for k, line in zip(order, lines):
        slab = both[:, at : at + len(line)].reshape(len(both), -1)
        found[k] = slab[:, : leaves[k].size].reshape(-1, *leaves[k].shape)
        at += len(line)
    numbers = iter(range(len(leaves)))
    return jax.tree.map(lambda _: found[next(numbers)], array)


def combined_pairwise(pieces, combine):
    while len(jax.tree.leaves(pieces)[0]) > 1:
        pieces = jax.vmap(combine)(
            *(jax.tree.map(lambda part: part[side::2], pieces) for side in (0, 1))
        )
    return jax.tree.map(lambda part: part[0], pieces)


def joined_all(array, axis, combine):
    pieces = gathered_once(array, axis)
    return combined_pairwise(pieces, combine)


def summed_on_arrival_2(array, axis, dim):
    pieces = split_up(array, dim, lax.axis_size(axis))
    arrived = lax.all_to_all(pieces, axis, split_axis=0, concat_axis=0, tiled=True)
    return arrived.sum(axis=0)


def per_device(
    main_queries, main_keys, log_sums, index_queries, index_weights, index_keys, loss_weights
):
    query_rows = index_queries.shape[0]
    key_rows = index_keys.shape[0]
    all_queries = main_queries.shape[0]
    local_heads = main_queries.shape[1]
    score_scale = main_queries.shape[2] ** (-0.5)
    block_count = all_queries // query_rows
    queries_blocks = main_queries.reshape(
        block_count, query_rows, local_heads, main_queries.shape[2]
    )
    logs_blocks = log_sums.reshape(block_count, query_rows, local_heads)

    def one_block(pieces):
        queries_block, logs_block = pieces
        scores = (
            jnp.einsum("qhd,khd->qhk", queries_block, main_keys, preferred_element_type=jnp.float32)
            * score_scale
        )
        return jnp.sum(jnp.exp(scores - logs_block[:, :, None]), axis=1)

    summed = lax.map(one_block, (queries_blocks, logs_blocks))
    probs = summed_on_arrival(summed.reshape(all_queries, key_rows).astype(jnp.bfloat16), "head", 0)
    queries_flat = index_queries.reshape(query_rows * IH, ID)
    raw_scores = jnp.dot(queries_flat, index_keys.T, preferred_element_type=jnp.float32).reshape(
        query_rows, IH, key_rows
    )
    positive = jnp.maximum(raw_scores, 0.0)
    weights_wide = index_weights.astype(jnp.float32)
    logits = jnp.sum(weights_wide[:, :, None] * positive, axis=1)
    local_top = jnp.max(logits, axis=1)
    local_mass = jnp.sum(probs, axis=1)

    def combine(former, latter):
        joint_top = jnp.maximum(former[0], latter[0])
        joint_total = former[1] * jnp.exp(former[0] - joint_top) + latter[1] * jnp.exp(
            latter[0] - joint_top
        )
        return (joint_top, joint_total, former[2] + latter[2])

    local_total = jnp.sum(jnp.exp(logits - local_top[:, None]), axis=1)
    row_top, row_total, row_mass = joined_all((local_top, local_total, local_mass), "ctx", combine)
    soft_share = jnp.exp(logits - row_top[:, None]) / row_total[:, None]
    target = probs / row_mass[:, None]
    grad_logits = (loss_weights[:, None] * (soft_share - target)).astype(jnp.bfloat16)
    grad_wide = grad_logits.astype(jnp.float32)
    weight_term = jnp.sum(grad_wide[:, None, :] * positive, axis=2)
    gated = jnp.where(raw_scores > 0, grad_wide[:, None, :] * weights_wide[:, :, None], 0.0).astype(
        jnp.bfloat16
    )
    gated_flat = gated.reshape(query_rows * IH, key_rows)
    owned = summed_on_arrival(
        jnp.einsum("qjk,kd->jqd", gated, index_keys, preferred_element_type=jnp.float32).astype(
            jnp.bfloat16
        ),
        "ctx",
        0,
    )
    query_grad = jnp.transpose(owned, (1, 0, 2))
    weight_grad = summed_on_arrival_2(weight_term, "ctx", 1)
    key_term = jnp.einsum("rk,rd->kd", gated_flat, queries_flat, preferred_element_type=jnp.float32)
    key_grad = summed_on_arrival(key_term.astype(jnp.bfloat16), "head", 1)
    return (query_grad.astype(jnp.bfloat16), weight_grad, key_grad.astype(jnp.bfloat16))


def solution(mesh):
    return jax.shard_map(
        per_device,
        mesh=mesh,
        in_specs=(
            P(None, "head", None),
            P("ctx", "head", None),
            P(None, "head"),
            P("head", None, None),
            P("head", None),
            P("ctx", None),
            P("head"),
        ),
        out_specs=(P("head", "ctx", None), P("head", "ctx"), P("ctx", "head")),
        check_vma=False,
    )
```

profile of v0, /device:TPU:8, one launch (start us, length us, event | category | flops | bytes accessed | tf_op | source)
XLA Modules:
  0.0 176.9 jit_solution(7224500171904888480)
XLA Ops:
  0.6 0.0 copy-start
  0.7 0.9 reshape.118
  1.6 7.7 %copy.13 = bf16[512,16,192]{2,1,0:T(8,128)(2,1)} copy(bf16[512,16,192]{0,2,1:T(8,128)(2,1)} %param.9) | data formatting | bytes 6291456 | tf_op args[0]
  9.3 0.0 copy-start.2
  9.3 0.0 copy-start.1
  9.3 50.5 %while.10 = (s32[]{:T(128)}, bf16[8,64,1024]{2,1,0:T(8,128)(2,1)}, bf16[8,64,16,192]{3,2,1,0:T(8,128)(2,1)}, bf16[1024,16,192]{0,2,1:T(8,128)(2,1)}, f32[8,64,16]{1,0,2:T(8,128)S(1)}, /*index=5*/s32[]{:T(128)}) while((s32[]{:T(128)}, bf16[8,64,1024]{2,1,0:T(8,128)(2,1)}, bf16[8,64,16,192]{3,2,1,0:T(8,128)(2,1)}, ...), condition=%wide.region_5.6_spmd, body=%wide.region_3.5_spmd.sunk | while | flops 405733376 | bytes 7876697 | solution.py:85
  9.3 1.1 constant_dynamic-slice_fusion.5
  10.4 4.5 %fusion.16 = bf16[64,1024]{1,0:T(8,128)(2,1)S(1)} fusion(bf16[1024,16,192]{0,2,1:T(8,128)(2,1)} %get-tuple-element.115, f32[64,16]{0,1:T(8,128)S(1)} %bitcast.70, bf16[1,64,16,192]{3,2,1,0:T(8,128)(2,1)S(1)} %constant_dynamic-slice_fusion.5), kind=kOutput, calls=%fused_computation.2.clone.1 | convolution fusion | flops 405733376 | bytes 6819840 | tf_op jit(solution)/shard_map/while/body/eval_jaxpr/qhd,khd->qhk/dot_general | solution.py:80
  14.9 0.7 bitcast_dynamic-update-slice_fusion.2
  15.6 1.1 constant_dynamic-slice_fusion.5
  16.7 4.5 %fusion.16 = bf16[64,1024]{1,0:T(8,128)(2,1)S(1)} fusion(bf16[1024,16,192]{0,2,1:T(8,128)(2,1)} %get-tuple-element.115, f32[64,16]{0,1:T(8,128)S(1)} %bitcast.70, bf16[1,64,16,192]{3,2,1,0:T(8,128)(2,1)S(1)} %constant_dynamic-slice_fusion.5), kind=kOutput, calls=%fused_computation.2.clone.1 | convolution fusion | flops 405733376 | bytes 6819840 | tf_op jit(solution)/shard_map/while/body/eval_jaxpr/qhd,khd->qhk/dot_general | solution.py:80
  21.2 0.7 bitcast_dynamic-update-slice_fusion.2
  21.9 1.1 constant_dynamic-slice_fusion.5
  23.0 4.5 %fusion.16 = bf16[64,1024]{1,0:T(8,128)(2,1)S(1)} fusion(bf16[1024,16,192]{0,2,1:T(8,128)(2,1)} %get-tuple-element.115, f32[64,16]{0,1:T(8,128)S(1)} %bitcast.70, bf16[1,64,16,192]{3,2,1,0:T(8,128)(2,1)S(1)} %constant_dynamic-slice_fusion.5), kind=kOutput, calls=%fused_computation.2.clone.1 | convolution fusion | flops 405733376 | bytes 6819840 | tf_op jit(solution)/shard_map/while/body/eval_jaxpr/qhd,khd->qhk/dot_general | solution.py:80
  27.5 0.7 bitcast_dynamic-update-slice_fusion.2
  28.2 1.1 constant_dynamic-slice_fusion.5
  29.3 4.5 %fusion.16 = bf16[64,1024]{1,0:T(8,128)(2,1)S(1)} fusion(bf16[1024,16,192]{0,2,1:T(8,128)(2,1)} %get-tuple-element.115, f32[64,16]{0,1:T(8,128)S(1)} %bitcast.70, bf16[1,64,16,192]{3,2,1,0:T(8,128)(2,1)S(1)} %constant_dynamic-slice_fusion.5), kind=kOutput, calls=%fused_computation.2.clone.1 | convolution fusion | flops 405733376 | bytes 6819840 | tf_op jit(solution)/shard_map/while/body/eval_jaxpr/qhd,khd->qhk/dot_general | solution.py:80
  33.9 0.7 bitcast_dynamic-update-slice_fusion.2
  34.5 1.1 constant_dynamic-slice_fusion.5
  35.6 4.5 %fusion.16 = bf16[64,1024]{1,0:T(8,128)(2,1)S(1)} fusion(bf16[1024,16,192]{0,2,1:T(8,128)(2,1)} %get-tuple-element.115, f32[64,16]{0,1:T(8,128)S(1)} %bitcast.70, bf16[1,64,16,192]{3,2,1,0:T(8,128)(2,1)S(1)} %constant_dynamic-slice_fusion.5), kind=kOutput, calls=%fused_computation.2.clone.1 | convolution fusion | flops 405733376 | bytes 6819840 | tf_op jit(solution)/shard_map/while/body/eval_jaxpr/qhd,khd->qhk/dot_general | solution.py:80
  40.2 0.7 bitcast_dynamic-update-slice_fusion.2
  40.8 1.1 constant_dynamic-slice_fusion.5
  41.9 4.5 %fusion.16 = bf16[64,1024]{1,0:T(8,128)(2,1)S(1)} fusion(bf16[1024,16,192]{0,2,1:T(8,128)(2,1)} %get-tuple-element.115, f32[64,16]{0,1:T(8,128)S(1)} %bitcast.70, bf16[1,64,16,192]{3,2,1,0:T(8,128)(2,1)S(1)} %constant_dynamic-slice_fusion.5), kind=kOutput, calls=%fused_computation.2.clone.1 | convolution fusion | flops 405733376 | bytes 6819840 | tf_op jit(solution)/shard_map/while/body/eval_jaxpr/qhd,khd->qhk/dot_general | solution.py:80
  46.5 0.7 bitcast_dynamic-update-slice_fusion.2
  47.1 1.1 constant_dynamic-slice_fusion.5
  48.2 4.5 %fusion.16 = bf16[64,1024]{1,0:T(8,128)(2,1)S(1)} fusion(bf16[1024,16,192]{0,2,1:T(8,128)(2,1)} %get-tuple-element.115, f32[64,16]{0,1:T(8,128)S(1)} %bitcast.70, bf16[1,64,16,192]{3,2,1,0:T(8,128)(2,1)S(1)} %constant_dynamic-slice_fusion.5), kind=kOutput, calls=%fused_computation.2.clone.1 | convolution fusion | flops 405733376 | bytes 6819840 | tf_op jit(solution)/shard_map/while/body/eval_jaxpr/qhd,khd->qhk/dot_general | solution.py:80
  52.8 0.7 bitcast_dynamic-update-slice_fusion.2
  53.4 1.1 constant_dynamic-slice_fusion.5
  54.5 4.5 %fusion.16 = bf16[64,1024]{1,0:T(8,128)(2,1)S(1)} fusion(bf16[1024,16,192]{0,2,1:T(8,128)(2,1)} %get-tuple-element.115, f32[64,16]{0,1:T(8,128)S(1)} %bitcast.70, bf16[1,64,16,192]{3,2,1,0:T(8,128)(2,1)S(1)} %constant_dynamic-slice_fusion.5), kind=kOutput, calls=%fused_computation.2.clone.1 | convolution fusion | flops 405733376 | bytes 6819840 | tf_op jit(solution)/shard_map/while/body/eval_jaxpr/qhd,khd->qhk/dot_general | solution.py:80
  59.1 0.7 bitcast_dynamic-update-slice_fusion.2
  59.7 0.0 copy-start.3
  59.7 5.8 %all-to-all-start = ((bf16[8,64,1024]{2,1,0:T(8,128)(2,1)}), bf16[8,64,1024]{2,1,0:T(8,128)(2,1)S(1)}, u32[]{:S(2)}, u32[]{:S(2)}) async-start(bf16[8,64,1024]{2,1,0:T(8,128)(2,1)} %get-tuple-element.30), calls=%async_computation | async-start | bytes 2097152 | tf_op jit(solution)/shard_map/all_to_all | solution.py:18
  65.5 0.0 copy-done.2
  65.5 0.0 copy-done
  65.5 0.0 copy-done.1
  65.5 7.0 %multiply_reduce_fusion.1 = (f32[64,1024]{1,0:T(8,128)S(1)}, f32[64,64,1024]{2,1,0:T(8,128)}) fusion(f32[64,64]{1,0:T(8,128)S(1)} %convert_element_type.43, bf16[64,64,128]{2,1,0:T(8,128)(2,1)S(1)} %copy-done, bf16[1024,128]{1,0:T(8,128)(2,1)S(1)} %copy-done.1), kind=kOutput, calls=%fused_computation.9 | convolution fusion | flops 1086259200 | bytes 18366464 | tf_op jit(solution)/shard_map/dot_general | solution.py:88
  72.5 0.1 reduce_max.9
  72.7 0.2 exponential_reduce_fusion
  72.9 7.1 %all-to-all-done = bf16[8,64,1024]{2,1,0:T(8,128)(2,1)S(1)} async-done(((bf16[8,64,1024]{2,1,0:T(8,128)(2,1)}), bf16[8,64,1024]{2,1,0:T(8,128)(2,1)S(1)}, u32[]{:S(2)}, u32[]{:S(2)}) %all-to-all-start) | async-done | bytes 1048608 | tf_op jit(solution)/shard_map/all_to_all | solution.py:18
  80.0 0.3 convert_reduce_fusion.1
  80.3 0.1 reshape.128
  80.4 20.3 %all_to_all.25 = f32[32,1,192]{2,1,0:T(1,128)S(1)} all-to-all(f32[32,1,192]{2,1,0:T(1,128)S(1)} %reshape.128), channel_id=1, replica_groups=mesh['head'=8,'ctx'=32] {'ctx'}, dimensions={0} | all-to-all | bytes 49152 | tf_op jit(solution)/shard_map/all_to_all | solution.py:24
  100.7 0.5 broadcast.42
  101.2 0.7 reduce.3
  102.0 0.1 reshape.129
  102.7 0.0 copy-done.3
  102.7 0.2 fusion.6
  102.8 7.5 %multiply_reduce_fusion = f32[64,64]{1,0:T(8,128)S(1)} fusion(f32[64,64,1024]{2,1,0:T(8,128)} %get-tuple-element.67, f32[64,1024]{1,0:T(8,128)S(1)} %fusion.6), kind=kLoop, calls=%fused_computation.7 | loop fusion | flops 12578816 | bytes 17055744 | tf_op jit(solution)/shard_map/reduce_sum | solution.py:110
  110.4 0.1 copy.18
  110.5 0.7 reshape.130
  111.2 3.8 %all-to-all-start.3 = ((f32[32,1,128]{2,1,0:T(1,128)}), f32[32,1,128]{2,1,0:T(1,128)S(1)}, u32[]{:S(2)}, u32[]{:S(2)}) async-start(f32[32,1,128]{2,1,0:T(1,128)} %reshape.130), calls=%async_computation.3 | async-start | bytes 32768 | tf_op jit(solution)/shard_map/all_to_all | solution.py:59
  115.0 7.6 %fusion.2 = bf16[1024,128]{0,1:T(8,128)(2,1)} fusion(bf16[64,64,128]{2,1,0:T(8,128)(2,1)S(1)} %copy-done, f32[64,64,1024]{2,1,0:T(8,128)} %get-tuple-element.67, f32[64,1024]{1,0:T(8,128)S(1)} %fusion.6, f32[64,64]{1,0:T(8,128)S(1)} %convert_element_type.43), kind=kOutput, calls=%fused_computation.14 | convolution fusion | flops 1090650112 | bytes 18366464 | tf_op jit(solution)/shard_map/rk,rd->kd/dot_general | solution.py:124
  122.6 2.1 %all-to-all-done.3 = f32[32,1,128]{2,1,0:T(1,128)S(1)} async-done(((f32[32,1,128]{2,1,0:T(1,128)}), f32[32,1,128]{2,1,0:T(1,128)S(1)}, u32[]{:S(2)}, u32[]{:S(2)}) %all-to-all-start.3) | async-done | bytes 16416 | tf_op jit(solution)/shard_map/all_to_all | solution.py:59
  124.7 4.8 %all-to-all-start.4 = ((bf16[8,1024,16]{1,2,0:T(8,128)(2,1)}), bf16[8,1024,16]{1,2,0:T(8,128)(2,1)S(1)}, u32[]{:S(2)}, u32[]{:S(2)}) async-start(bf16[8,1024,16]{1,2,0:T(8,128)(2,1)} %bitcast.22), calls=%async_computation.4 | async-start | bytes 524288 | tf_op jit(solution)/shard_map/all_to_all | solution.py:18
  129.5 7.1 %convolution_convert_fusion = bf16[64,64,128]{2,1,0:T(8,128)(2,1)S(1)} fusion(f32[64,64,1024]{2,1,0:T(8,128)} %get-tuple-element.67, f32[64,1024]{1,0:T(8,128)S(1)} %fusion.6, f32[64,64]{1,0:T(8,128)S(1)} %convert_element_type.43, bf16[1024,128]{1,0:T(8,128)(2,1)S(1)} %copy-done.1), kind=kOutput, calls=%fused_computation.12 | convolution fusion | flops 1091043328 | bytes 18366464 | tf_op jit(solution)/shard_map/qjk,kd->jqd/dot_general | solution.py:116
  136.7 2.1 %copy.17 = bf16[32,2,64,128]{3,1,2,0:T(2,128)(2,1)} copy(bf16[32,2,64,128]{3,1,0,2:T(2,128)(2,1)S(1)} %bitcast.69) | data formatting | bytes 2097152 | tf_op jit(solution)/shard_map/reshape | solution.py:12
  138.8 0.0 all-to-all-done.4
  138.8 7.7 %all-to-all-start.2 = ((bf16[32,2,64,128]{3,1,2,0:T(2,128)(2,1)}), bf16[32,2,64,128]{3,1,2,0:T(2,128)(2,1)S(1)}, u32[]{:S(2)}, u32[]{:S(2)}) async-start(bf16[32,2,64,128]{3,1,2,0:T(2,128)(2,1)} %copy.17), calls=%async_computation.2 | async-start | bytes 2097152 | tf_op jit(solution)/shard_map/all_to_all | solution.py:18
  146.4 0.7 reduce.4
  147.1 0.1 reshape.131
  147.2 0.6 bitcast_reduce_fusion
  147.8 0.7 reduce_sum.94
  148.5 26.8 %all-to-all-done.2 = bf16[32,2,64,128]{3,1,2,0:T(2,128)(2,1)S(1)} async-done(((bf16[32,2,64,128]{3,1,2,0:T(2,128)(2,1)}), bf16[32,2,64,128]{3,1,2,0:T(2,128)(2,1)S(1)}, u32[]{:S(2)}, u32[]{:S(2)}) %all-to-all-start.2) | async-done | bytes 1048608 | tf_op jit(solution)/shard_map/all_to_all | solution.py:18
  175.3 1.6 reduce_sum.91
  (46 shorter events, 0.7 us)
Async XLA Ops:
  0.6 64.9 %copy-start = (bf16[64,64,128]{2,1,0:T(8,128)(2,1)S(1)}, bf16[64,64,128]{2,1,0:T(8,128)(2,1)}, u32[]{:S(2)}) copy-start(bf16[64,64,128]{2,1,0:T(8,128)(2,1)} %param.12) | copy-start | bytes 3145732
  9.3 56.2 %copy-start.2 = (bf16[64,64]{1,0:T(8,128)(2,1)S(1)}, bf16[64,64]{1,0:T(8,128)(2,1)}, u32[]{:S(2)}) copy-start(bf16[64,64]{1,0:T(8,128)(2,1)} %param.13) | copy-start | bytes 24580
  9.3 56.2 %copy-start.1 = (bf16[1024,128]{1,0:T(8,128)(2,1)S(1)}, bf16[1024,128]{1,0:T(8,128)(2,1)}, u32[]{:S(2)}) copy-start(bf16[1024,128]{1,0:T(8,128)(2,1)} %param.14) | copy-start | bytes 786436
  59.7 43.0 %copy-start.3 = (f32[64]{0:T(128)S(1)}, f32[64]{0:T(128)}, u32[]{:S(2)}) copy-start(f32[64]{0:T(128)} %param.15) | copy-start | bytes 772
  59.7 20.3 %all-to-all-start = ((bf16[8,64,1024]{2,1,0:T(8,128)(2,1)}), bf16[8,64,1024]{2,1,0:T(8,128)(2,1)S(1)}, u32[]{:S(2)}, u32[]{:S(2)}) async-start(bf16[8,64,1024]{2,1,0:T(8,128)(2,1)} %get-tuple-element.30), calls=%async_computation | async-start | bytes 2097152 | tf_op jit(solution)/shard_map/all_to_all | solution.py:18
  111.2 13.6 %all-to-all-start.3 = ((f32[32,1,128]{2,1,0:T(1,128)}), f32[32,1,128]{2,1,0:T(1,128)S(1)}, u32[]{:S(2)}, u32[]{:S(2)}) async-start(f32[32,1,128]{2,1,0:T(1,128)} %reshape.130), calls=%async_computation.3 | async-start | bytes 32768 | tf_op jit(solution)/shard_map/all_to_all | solution.py:59
  124.7 14.0 %all-to-all-start.4 = ((bf16[8,1024,16]{1,2,0:T(8,128)(2,1)}), bf16[8,1024,16]{1,2,0:T(8,128)(2,1)S(1)}, u32[]{:S(2)}, u32[]{:S(2)}) async-start(bf16[8,1024,16]{1,2,0:T(8,128)(2,1)} %bitcast.22), calls=%async_computation.4 | async-start | bytes 524288 | tf_op jit(solution)/shard_map/all_to_all | solution.py:18
  138.8 36.6 %all-to-all-start.2 = ((bf16[32,2,64,128]{3,1,2,0:T(2,128)(2,1)}), bf16[32,2,64,128]{3,1,2,0:T(2,128)(2,1)S(1)}, u32[]{:S(2)}, u32[]{:S(2)}) async-start(bf16[32,2,64,128]{3,1,2,0:T(2,128)(2,1)} %copy.17), calls=%async_computation.2 | async-start | bytes 2097152 | tf_op jit(solution)/shard_map/all_to_all | solution.py:18
where the time goes:
time: 178 us; the launch traced here: 177 us
  matrix products  58 us (33%)
  waiting for transfers between devices  36.1 us (20%)
  local copies, waits for them, and re-layouts  26.9 us (15%)
  starting transfers between devices  22 us (12%)
  blocking collectives  20.3 us (11%)
  other arithmetic  12.7 us (7%)
    dot_general x8, matrix products, one_block(): jnp.einsum('qhd,khd->qhk', queries_block, main_keys, preferred_element_ty...  36.2 us
    all_to_all x3, waiting for transfers between devices, summed_on_arrival(): lax.all_to_all(pieces, axis, split_axis=0, concat_axis=0, tiled=True)  34 us
    all_to_all x1, blocking collectives, from_everyone(): return lax.all_to_all(copies, axis, split_axis=0, concat_axis=0, tiled=True)  20.3 us
    all_to_all x3, starting transfers between devices, summed_on_arrival(): lax.all_to_all(pieces, axis, split_axis=0, concat_axis=0, tiled=True)  18.2 us
    dynamic_slice x16, local copies, waits for them, and re-layouts, per_device(): summed = lax.map(one_block, (queries_blocks, logs_blocks))  8.79 us
    unnamed x13, local copies, waits for them, and re-layouts  8.68 us
    dot_general x1, matrix products, per_device(): jnp.einsum('rk,rd->kd', gated_flat, queries_flat, preferred_element_type=...  7.62 us
    reduce_sum x1, other arithmetic, per_device(): weight_term = jnp.sum(grad_wide[:, None, :] * positive, axis=2)  7.53 us
  transfers between devices with their start and end apart: 4, of which 3 were waited for; matrix products, arithmetic and copies ran while one was open for 15% of the time, Pallas kernels for 0%

commit v1 on v0

v1 whole, which is shorter than its diff:
```python
import functools
import math

import jax
import jax.numpy as jnp
from jax import lax
from jax.experimental import pallas as pl
from jax.experimental.pallas import tpu as pltpu
from jax.sharding import Mesh, PartitionSpec as P

F32 = jnp.float32
BF16 = jnp.bfloat16
NY, NC, NX, NZ = 4, 2, 4, 8
MIB = 1 << 20


def rotate(array, axis, shift):
    n = lax.axis_size(axis)
    return lax.ppermute(array, axis, [(i, (i + shift) % n) for i in range(n)])


def score_kernel(place, queries, keys, logs, keep, send, total, *, heads, rows, scale):
    head = pl.program_id(0)

    @pl.when(head == 0)
    def _():
        total[...] = jnp.zeros_like(total)

    depth = queries.shape[1]
    cols = queries.shape[2]
    log_row = logs[0] * (-1.0 / scale)
    high = log_row.astype(BF16).astype(F32)
    rest = log_row - high
    middle = rest.astype(BF16).astype(F32)
    low = rest - middle
    line = lax.broadcasted_iota(jnp.int32, (16, cols), 0)
    extra = jnp.where(
        line == 0, high, jnp.where(line == 1, middle, jnp.where(line == 2, low, 0.0))
    ).astype(BF16)
    left = jnp.concatenate([queries[0], extra], axis=0).T
    right = jnp.concatenate([keys[0], jnp.ones((16, keys.shape[2]), BF16)], axis=0)
    factor = scale * math.log2(math.e)
    tile = 128
    for at in range(0, cols, tile):
        scores = jnp.dot(left[at : at + tile], right, preferred_element_type=F32)
        total[at : at + tile, :] += jnp.exp2(scores * factor)

    @pl.when(head == heads - 1)
    def _():
        y, core = place[0], place[1]
        for r in range(NY):
            base = lax.rem(y + r, NY) * (NC * rows)
            mine = pl.multiple_of(base + core * rows, rows)
            other = pl.multiple_of(base + (1 - core) * rows, rows)
            keep[r] = total[pl.ds(mine, rows), :].astype(BF16)
            send[r] = total[pl.ds(other, rows), :].astype(BF16)


def head_scores(place, queries, keys, logs, rows, scale):
    heads, depth, count = queries.shape
    width = keys.shape[2]
    out = jax.ShapeDtypeStruct((NY, rows, width), BF16)
    whole = pl.BlockSpec((NY, rows, width), lambda h, p: (0, 0, 0))
    return pl.pallas_call(
        functools.partial(score_kernel, heads=heads, rows=rows, scale=scale),
        grid_spec=pltpu.PrefetchScalarGridSpec(
            num_scalar_prefetch=1,
            grid=(heads,),
            in_specs=[
                pl.BlockSpec((1, depth, count), lambda h, p: (h, 0, 0)),
                pl.BlockSpec((1, depth, width), lambda h, p: (h, 0, 0)),
                pl.BlockSpec((1, 1, count), lambda h, p: (h, 0, 0)),
            ],
            out_specs=[whole, whole],
            scratch_shapes=[pltpu.VMEM((count, width), F32)],
        ),
        out_shape=[out, out],
        compiler_params=pltpu.CompilerParams(vmem_limit_bytes=32 * MIB),
        cost_estimate=pl.CostEstimate(
            flops=2 * heads * depth * count * width,
            bytes_accessed=12 * MIB,
            transcendentals=heads * count * width,
        ),
        name="head_scores",
    )(place, queries, keys, logs[:, None, :])


def logit_kernel(queries, keys, weights, logits, mask, *, group):
    step = pl.program_id(0)
    rows = queries.shape[1]

    @pl.when(step == 0)
    def _():
        logits[...] = jnp.zeros_like(logits)

    for k in range(group):
        raw = lax.dot_general(
            queries[k], keys[...], (((1,), (1,)), ((), ())), preferred_element_type=F32
        )
        mask[k] = jnp.where(raw > 0, 1.0, 0.0).astype(BF16)
        logits[...] += weights[k] * jnp.maximum(raw, 0.0)


def index_logits(queries, keys, weights):
    heads, rows, depth = queries.shape
    width = keys.shape[0]
    group = 8
    return pl.pallas_call(
        functools.partial(logit_kernel, group=group),
        grid=(heads // group,),
        in_specs=[
            pl.BlockSpec((group, rows, depth), lambda i: (i, 0, 0)),
            pl.BlockSpec((width, depth), lambda i: (0, 0)),
            pl.BlockSpec((group, rows, 1), lambda i: (i, 0, 0)),
        ],
        out_specs=[
            pl.BlockSpec((rows, width), lambda i: (0, 0)),
            pl.BlockSpec((group, rows, width), lambda i: (i, 0, 0)),
        ],
        out_shape=[
            jax.ShapeDtypeStruct((rows, width), F32),
            jax.ShapeDtypeStruct((heads, rows, width), BF16),
        ],
        compiler_params=pltpu.CompilerParams(vmem_limit_bytes=32 * MIB),
        cost_estimate=pl.CostEstimate(
            flops=2 * heads * rows * depth * width,
            bytes_accessed=10 * MIB,
            transcendentals=0,
        ),
        name="index_logits",
    )(queries, keys, weights)


def stats_kernel(logits, one, two, three, four, probs, stats):
    summed = (
        one[...].astype(F32) + two[...].astype(F32) + three[...].astype(F32) + four[...].astype(F32)
    )
    probs[...] = summed
    values = logits[...]
    top = jnp.max(values, axis=1, keepdims=True)
    total = jnp.sum(jnp.exp(values - top), axis=1, keepdims=True)
    mass = jnp.sum(summed, axis=1, keepdims=True)
    lane = lax.broadcasted_iota(jnp.int32, (values.shape[0], 128), 1)
    packed = jnp.where(lane == 0, top, jnp.where(lane == 1, total, jnp.where(lane == 2, mass, 0.0)))
    stats[...] = packed.T[:8]


def local_stats(logits, parts):
    rows, width = logits.shape
    return pl.pallas_call(
        stats_kernel,
        out_shape=[
            jax.ShapeDtypeStruct((rows, width), F32),
            jax.ShapeDtypeStruct((8, rows), F32),
        ],
        compiler_params=pltpu.CompilerParams(vmem_limit_bytes=16 * MIB),
        name="local_stats",
    )(logits, *parts)


def grad_kernel(place, logits, probs, stats, loss, mask, keys, scaled, query_part, key_part, grads, total, *, steps):
    step = pl.program_id(0)
    rows = logits.shape[0]

    @pl.when(step == 0)
    def _():
        each = stats[...]
        tops = each[:, 0, :]
        top = jnp.max(tops, axis=0, keepdims=True)
        denominator = jnp.sum(each[:, 1, :] * jnp.exp(tops - top), axis=0, keepdims=True)
        mass = jnp.sum(each[:, 2, :], axis=0, keepdims=True)
        line = lax.broadcasted_iota(jnp.int32, (128, rows), 0)
        packed = jnp.where(
            line == 0,
            top,
            jnp.where(line == 1, denominator, jnp.where(line == 2, mass, loss[...])),
        ).T
        soft = jnp.exp(logits[...] - packed[:, 0:1]) / packed[:, 1:2]
        target = probs[...] / packed[:, 2:3]
        grads[...] = (packed[:, 3:4] * (soft - target)).astype(BF16)
        total[...] = jnp.zeros_like(total)

    group = mask.shape[0]
    width = mask.shape[2]
    half = group // 4
    values = grads[...]
    for at in range(0, group, half):
        gated = (mask[at : at + half] * values[None]).reshape(half * rows, width)
        query_part[0, at : at + half] = (
            jnp.dot(gated, keys[...], preferred_element_type=F32)
            .astype(BF16)
            .reshape(half, rows, keys.shape[1])
        )
        left = scaled[at : at + half].reshape(half * rows, keys.shape[1])
        total[...] += lax.dot_general(
            left, gated, (((0,), (0,)), ((), ())), preferred_element_type=F32
        )

    @pl.when(step == steps - 1)
    def _():
        key_part[...] = total[...].astype(BF16)


def gradients(place, logits, probs, stats, loss, mask, keys, scaled):
    heads, rows, width = mask.shape
    depth = keys.shape[1]
    group = heads // NX
    turn = lambda i, p: (lax.rem(p[2] + i, NX), 0, 0)
    fixed2 = lambda i, p: (0, 0)
    return pl.pallas_call(
        functools.partial(grad_kernel, steps=NX),
        grid_spec=pltpu.PrefetchScalarGridSpec(
            num_scalar_prefetch=1,
            grid=(NX,),
            in_specs=[
                pl.BlockSpec((rows, width), fixed2),
                pl.BlockSpec((rows, width), fixed2),
                pl.BlockSpec(stats.shape, lambda i, p: (0, 0, 0)),
                pl.BlockSpec((1, rows), fixed2),
                pl.BlockSpec((group, rows, width), turn),
                pl.BlockSpec((width, depth), fixed2),
                pl.BlockSpec((group, rows, depth), turn),
            ],
            out_specs=[
                pl.BlockSpec((1, group, rows, depth), lambda i, p: (i, 0, 0, 0)),
                pl.BlockSpec((depth, width), fixed2),
            ],
            scratch_shapes=[pltpu.VMEM((rows, width), BF16), pltpu.VMEM((depth, width), F32)],
        ),
        out_shape=[
            jax.ShapeDtypeStruct((NX, group, rows, depth), BF16),
            jax.ShapeDtypeStruct((depth, width), BF16),
        ],
        compiler_params=pltpu.CompilerParams(vmem_limit_bytes=40 * MIB),
        cost_estimate=pl.CostEstimate(
            flops=4 * heads * rows * depth * width, bytes_accessed=12 * MIB, transcendentals=0
        ),
        name="gradients",
    )(place, logits, probs, stats, loss, mask, keys, scaled)


def per_device(
    main_queries, main_keys, log_sums, index_queries, index_weights, index_keys, loss_weights
):
    rows, heads, depth = index_queries.shape
    width = index_keys.shape[0]
    scale = main_queries.shape[2] ** (-0.5)
    x, z = lax.axis_index("x"), lax.axis_index("z")
    place = jnp.stack([lax.axis_index("y"), lax.axis_index("core"), x]).astype(jnp.int32)

    keep, send = head_scores(
        place,
        jnp.transpose(main_queries, (1, 2, 0)),
        jnp.transpose(main_keys, (1, 2, 0)),
        log_sums.T,
        rows,
        scale,
    )
    arrived = rotate(send, "core", 1)
    pairs = [(keep[r].astype(F32) + arrived[r].astype(F32)).astype(BF16) for r in range(NY)]
    parts = [pairs[0]] + [rotate(pairs[r], "y", r) for r in range(1, NY)]

    turned = jnp.transpose(index_queries, (1, 0, 2))
    weight_columns = index_weights.T.astype(F32)[:, :, None]
    logits, mask = index_logits(turned, index_keys, weight_columns)
    scaled = (turned.astype(F32) * weight_columns).astype(BF16)

    probs, stats = local_stats(logits, parts)
    everywhere = lax.all_to_all(
        jnp.broadcast_to(stats[None], (NX * NZ, *stats.shape)),
        ("x", "z"),
        split_axis=0,
        concat_axis=0,
        tiled=True,
    )
    query_part, key_part = gradients(
        place, logits, probs, everywhere, loss_weights[None], mask, index_keys, scaled
    )
    across = [query_part[0]] + [rotate(query_part[r], "x", r) for r in range(1, NX)]
    summed = sum(part.astype(F32) for part in across).astype(BF16)
    pieces = lax.all_to_all(
        summed.reshape(NZ, heads // (NX * NZ), rows, depth),
        "z",
        split_axis=0,
        concat_axis=0,
        tiled=True,
    )
    owned = pieces.astype(F32).sum(axis=0)
    mine = heads // (NX * NZ)
    first = (x * NZ + z) * mine
    own_queries = lax.dynamic_slice_in_dim(turned, first, mine, 0).astype(F32)
    own_weights = lax.dynamic_slice_in_dim(weight_columns, first, mine, 0)
    query_grad = jnp.transpose((owned * own_weights).astype(BF16), (1, 0, 2))
    weight_grad = jnp.sum(owned * own_queries, axis=2).T

    key_pieces = lax.all_to_all(
        key_part.reshape(NY * NC, depth // (NY * NC), width),
        ("y", "core"),
        split_axis=0,
        concat_axis=0,
        tiled=True,
    )
    key_grad = key_pieces.astype(F32).sum(axis=0).astype(BF16).T
    return query_grad, weight_grad, key_grad


def solution(mesh):
    fine = Mesh(mesh.devices.reshape(NY, NC, NX, NZ), ("y", "core", "x", "z"))
    head, ctx = ("y", "core"), ("x", "z")
    return jax.shard_map(
        per_device,
        mesh=fine,
        in_specs=(
            P(None, head, None),
            P(ctx, head, None),
            P(None, head),
            P(head, None, None),
            P(head, None),
            P(ctx, None),
            P(head),
        ),
        out_specs=(P(head, ctx, None), P(head, ctx), P(ctx, head)),
        check_vma=False,
    )
```

time: 178 us -> 106 us (0.60)
  matrix products: 58 us -> 0 us
  Pallas kernels: 0 us -> 22.2 us
  blocking collectives: 20.3 us -> 0 us
  waiting for transfers between devices: 36.1 us -> 25.5 us
  other arithmetic: 12.7 us -> 5.93 us
  starting transfers between devices: 22 us -> 28.5 us
  local copies, waits for them, and re-layouts: 26.9 us -> 21.7 us
    dot_general x11 -> x0, matrix products: 58 us -> none  [the longest x8 36.2 us: one_block(): jnp.einsum('qhd,khd->qhk', queries_block, main_keys, preferred_element_ty...]
    pallas_call x0 -> x4, Pallas kernels: none -> 22.2 us  [the longest x1 8.88 us: head_scores(): pl.pallas_call(functools.partial(score_kernel, heads=heads, rows=rows, sc...]
    all_to_all x1 -> x0, blocking collectives: 20.3 us -> none  [from_everyone(): return lax.all_to_all(copies, axis, split_axis=0, concat_axis=0, tiled=True)]
    all_to_all x4 -> x3, waiting for transfers between devices: 36.1 us -> 18.6 us  [the longest x1 10.3 us: per_device(): lax.all_to_all(summed.reshape(NZ, heads // (NX * NZ), rows, depth), 'z',...]
    reduce_sum x6 -> x3, other arithmetic: 10.9 us -> 0.8 us  [the longest x1 0.65 us: per_device(): key_grad = key_pieces.astype(F32).sum(axis=0).astype(BF16).T]
    unnamed x13 -> x29, local copies, waits for them, and re-layouts: 8.68 us -> 18.2 us
    ppermute x0 -> x7, starting transfers between devices: none -> 9.03 us  [rotate(): return lax.ppermute(array, axis, [(i, (i + shift) % n) for i in range(n)])]
    dynamic_slice x16 -> x0, local copies, waits for them, and re-layouts: 8.79 us -> none  [per_device(): summed = lax.map(one_block, (queries_blocks, logs_blocks))]
  transfers between devices with their start and end apart: 4 -> 10, of which waited for: 3 -> 6; matrix products, arithmetic and copies ran while one was open for 15% -> 7% of each run, Pallas kernels for 0% -> 7%
where the time goes in v1:
time: 106 us; the launch traced here: 105 us
  starting transfers between devices  28.5 us (27%)
  waiting for transfers between devices  25.5 us (24%)
  Pallas kernels  22.2 us (21%)
  local copies, waits for them, and re-layouts  21.7 us (20%)
  other arithmetic  5.93 us (6%)
    unnamed x29, local copies, waits for them, and re-layouts  18.2 us
    all_to_all x1, starting transfers between devices, per_device(): lax.all_to_all(jnp.broadcast_to(stats[None], (NX * NZ, *stats.shape)), ('...  11.4 us
    all_to_all x1, waiting for transfers between devices, per_device(): lax.all_to_all(summed.reshape(NZ, heads // (NX * NZ), rows, depth), 'z',...  10.3 us
    ppermute x7, starting transfers between devices, rotate(): return lax.ppermute(array, axis, [(i, (i + shift) % n) for i in range(n)])  9.03 us
    pallas_call x1, Pallas kernels, head_scores(): pl.pallas_call(functools.partial(score_kernel, heads=heads, rows=rows, sc...  8.88 us
    all_to_all x1, waiting for transfers between devices, per_device(): lax.all_to_all(jnp.broadcast_to(stats[None], (NX * NZ, *stats.shape)), ('...  8.17 us
    pallas_call x1, Pallas kernels, index_logits(): pl.pallas_call(functools.partial(logit_kernel, group=group), grid=(heads...  7.18 us
    ppermute x7, waiting for transfers between devices, rotate(): return lax.ppermute(array, axis, [(i, (i + shift) % n) for i in range(n)])  6.92 us
  transfers between devices with their start and end apart: 10, of which 6 were waited for; matrix products, arithmetic and copies ran while one was open for 7% of the time, Pallas kernels for 7%

profile of v1, /device:TPU:8, one launch (start us, length us, event | category | flops | bytes accessed | tf_op | source)
XLA Modules:
  0.0 104.6 jit_solution(9495757206951131637)
XLA Ops:
  0.6 0.8 broadcast_in_dim.16.logs
  1.4 0.1 pad_add_fusion.place
  1.5 0.0 copy-start.8
  1.5 2.8 %copy-done.8 = bf16[1024,16,192]{0,2,1:T(8,128)(2,1)S(1)} copy-done((bf16[1024,16,192]{0,2,1:T(8,128)(2,1)S(1)}, bf16[1024,16,192]{0,2,1:T(8,128)(2,1)}, u32[]{:S(2)}) %copy-start.8) | copy-done | bytes 6291480
  4.3 0.0 copy-start.9
  4.3 1.9 %copy-done.9 = bf16[512,16,192]{0,2,1:T(8,128)(2,1)S(1)} copy-done((bf16[512,16,192]{0,2,1:T(8,128)(2,1)S(1)}, bf16[512,16,192]{0,2,1:T(8,128)(2,1)}, u32[]{:S(2)}) %copy-start.9) | copy-done | bytes 3145752
  6.2 0.0 copy-start.10
  6.2 8.9 %head_scores.1 = (bf16[4,64,1024]{2,1,0:T(8,128)(2,1)S(1)}, bf16[4,64,1024]{2,1,0:T(8,128)(2,1)S(1)}) custom-call(s32[3]{0:T(128)S(1)} %pad_add_fusion.place, bf16[16,192,512]{2,1,0:T(8,128)(2,1)S(1)} %bitcast.48, bf16[16,192,1024]{2,1,0:T(8,128)(2,1)S(1)} %bitcast.47, f32[16,1,512]{2,1,0:T(1,128)S(1)} %broadcast_in_dim.16.logs), custom_call_target="tpu_custom_call" | custom-call | flops 3221225472 | bytes 12582912 | tf_op jit(solution)/shard_map/head_scores/pallas_call | solution.py:64
  15.1 0.1 collective-permute-start
  15.2 0.0 copy-done.10
  15.2 0.1 copy.18
  15.3 1.8 %collective-permute-done = bf16[4,64,1024]{2,1,0:T(8,128)(2,1)S(1)} collective-permute-done((bf16[4,64,1024]{2,1,0:T(8,128)(2,1)S(1)}, bf16[4,64,1024]{2,1,0:T(8,128)(2,1)S(1)}, u32[]{:S(2)}, u32[]{:S(2)}) %collective-permute-start) | collective-permute-done | bytes 524320 | tf_op jit(solution)/shard_map/ppermute | solution.py:19
  17.1 0.9 fusion.6
  17.9 1.6 %collective-permute-start.1 = (bf16[64,1024]{1,0:T(8,128)(2,1)}, bf16[64,1024]{1,0:T(8,128)(2,1)}, u32[]{:S(2)}, u32[]{:S(2)}) collective-permute-start(bf16[64,1024]{1,0:T(8,128)(2,1)} %get-tuple-element.29), channel_id=1, source_target_pairs={{0,64},{64,128},{128,192},{192,0},{1,65},{65,129},{129,193},{193,1... | collective-permute-start | bytes 393224 | tf_op jit(solution)/shard_map/ppermute | solution.py:19
  19.5 2.6 %collective-permute-start.2 = (bf16[64,1024]{1,0:T(8,128)(2,1)}, bf16[64,1024]{1,0:T(8,128)(2,1)}, u32[]{:S(2)}, u32[]{:S(2)}) collective-permute-start(bf16[64,1024]{1,0:T(8,128)(2,1)} %get-tuple-element.28), channel_id=1, source_target_pairs={{0,128},{64,192},{128,0},{192,64},{1,129},{65,193},{129,1},{193,65... | collective-permute-start | bytes 393224 | tf_op jit(solution)/shard_map/ppermute | solution.py:19
  22.2 0.7 collective-permute-start.3
  22.9 0.6 fusion.10
  23.5 0.7 copy.19.weights
  24.2 0.0 copy-start.2
  24.2 1.9 %copy.28 = bf16[64,64,128]{2,0,1:T(8,128)(2,1)S(1)} copy(bf16[64,64,128]{2,1,0:T(8,128)(2,1)} %param.10) | data formatting | bytes 2097152 | tf_op args[3]
  26.1 0.0 copy-done.2
  26.2 7.2 %index_logits.1 = (f32[64,1024]{1,0:T(8,128)S(1)}, bf16[64,64,1024]{2,1,0:T(8,128)(2,1)S(1)}) custom-call(bf16[64,64,128]{2,1,0:T(8,128)(2,1)S(1)} %bitcast.44, bf16[1024,128]{1,0:T(8,128)(2,1)S(1)} %copy-done.2, f32[64,64,1]{2,1,0:T(8,128)S(1)} %copy.19.weights), custom_call_target="tpu_custom_call" | custom-call | flops 1073741824 | bytes 10485760 | tf_op jit(solution)/shard_map/index_logits/pallas_call | solution.py:108
  33.3 0.0 copy-start
  33.4 3.2 %copy-done = bf16[64,64,1024]{2,1,0:T(8,128)(2,1)} copy-done((bf16[64,64,1024]{2,1,0:T(8,128)(2,1)}, bf16[64,64,1024]{2,1,0:T(8,128)(2,1)S(1)}, u32[]{:S(2)}) %copy-start) | copy-done | bytes 8388632
  36.6 0.0 collective-permute-done.1.two
  36.6 0.0 collective-permute-done.2.three
  36.6 0.0 collective-permute-done.3.four
  36.6 1.3 %local_stats.1 = (f32[64,1024]{1,0:T(8,128)S(1)}, f32[8,64]{1,0:T(8,128)S(1)}) custom-call(f32[64,1024]{1,0:T(8,128)S(1)} %get-tuple-element.11.logits, bf16[64,1024]{1,0:T(8,128)(2,1)S(1)} %get-tuple-element.30.one, bf16[64,1024]{1,0:T(8,128)(2,1)} %collective-permute-done.1.two, bf16[64,1024]{1,0:T(8,128)(2,1)} %collective-permute-done.2.three, ...), custom_call_target="tpu_custom_call" | custom-call | tf_op jit(solution)/shard_map/local_stats/pallas_call | solution.py:150
  37.9 0.0 copy-start.4
  37.9 0.7 copy-done.4
  38.6 0.7 reshape.37
  39.4 11.4 %all-to-all-start = ((f32[32,1,512]{2,1,0:T(1,128)}), f32[32,1,512]{2,1,0:T(1,128)S(1)}, u32[]{:S(2)}, u32[]{:S(2)}) async-start(f32[32,1,512]{2,1,0:T(1,128)} %reshape.37), calls=%async_computation | async-start | bytes 131072 | tf_op jit(solution)/shard_map/all_to_all | solution.py:269
  50.7 1.8 %multiply_convert_fusion.scaled = bf16[64,64,128]{2,1,0:T(8,128)(2,1)S(1)} fusion(f32[64,64]{1,0:T(8,128)} %get-tuple-element.32, bf16[64,64,128]{2,1,0:T(8,128)(2,1)} %param.10), kind=kLoop, calls=%fused_computation | loop fusion | flops 1572864 | bytes 2113536 | tf_op jit(solution)/shard_map/convert_element_type | solution.py:266
  52.5 8.2 %all-to-all-done = f32[32,1,512]{2,1,0:T(1,128)S(1)} async-done(((f32[32,1,512]{2,1,0:T(1,128)}), f32[32,1,512]{2,1,0:T(1,128)S(1)}, u32[]{:S(2)}, u32[]{:S(2)}) %all-to-all-start) | async-done | bytes 65568 | tf_op jit(solution)/shard_map/all_to_all | solution.py:269
  60.7 0.5 broadcast.3
  61.2 0.8 reduce.1
  62.0 0.1 reshape.38.stats
  62.1 0.0 copy-done.7
  62.1 0.0 copy-start.1
  62.1 3.4 %copy-done.1 = bf16[64,64,1024]{2,1,0:T(8,128)(2,1)S(1)} copy-done((bf16[64,64,1024]{2,1,0:T(8,128)(2,1)S(1)}, bf16[64,64,1024]{2,1,0:T(8,128)(2,1)}, u32[]{:S(2)}) %copy-start.1) | copy-done | bytes 8388632
  65.5 0.9 copy-done.3
  66.5 0.9 copy-done.5
  67.4 4.8 %gradients.1 = (bf16[4,16,64,128]{3,2,1,0:T(8,128)(2,1)S(1)}, bf16[128,1024]{1,0:T(8,128)(2,1)S(1)}) custom-call(s32[3]{0:T(128)S(1)} %pad_add_fusion.place, f32[64,1024]{1,0:T(8,128)S(1)} %get-tuple-element.11.logits, f32[64,1024]{1,0:T(8,128)S(1)} %copy-done.5, f32[32,8,64]{2,1,0:T(8,128)S(1)} %reshape.38.stats, f32[1,64]{1,0:T(1,128)S(1)} %bitcast.46, ...), custom_call_target="tpu_custom_call" | custom-call | flops 2147483648 | bytes 12582912 | tf_op jit(solution)/shard_map/gradients/pallas_call | solution.py:210
  72.2 0.0 copy-start.6
  72.2 0.9 slice_bitcast_fusion.2
  73.1 0.6 collective-permute-start.4
  73.8 2.0 %collective-permute-start.5 = (bf16[16,64,128]{2,1,0:T(8,128)(2,1)}, bf16[16,64,128]{2,1,0:T(8,128)(2,1)S(1)}, u32[]{:S(2)}, u32[]{:S(2)}) collective-permute-start(bf16[16,64,128]{2,1,0:T(8,128)(2,1)} %get-tuple-element.26), channel_id=1, source_target_pairs={{0,16},{8,24},{16,0},{24,8},{1,17},{9,25},{17,1},{25,9},{2,18},{10... | collective-permute-start | bytes 786440 | tf_op jit(solution)/shard_map/ppermute | solution.py:19
  75.8 1.3 %collective-permute-start.6 = (bf16[16,64,128]{2,1,0:T(8,128)(2,1)S(1)}, bf16[16,64,128]{2,1,0:T(8,128)(2,1)S(1)}, u32[]{:S(2)}, u32[]{:S(2)}) collective-permute-start(bf16[16,64,128]{2,1,0:T(8,128)(2,1)S(1)} %get-tuple-element.25), channel_id=1, source_target_pairs={{0,24},{8,0},{16,8},{24,16},{1,25},{9,1},{17,9},{25,17},{2,26},{10... | collective-permute-start | bytes 786440 | tf_op jit(solution)/shard_map/ppermute | solution.py:19
  77.1 0.0 copy-done.6
  77.1 4.7 %all-to-all-start.2 = ((bf16[8,16,1024]{2,1,0:T(8,128)(2,1)}), bf16[8,16,1024]{2,1,0:T(8,128)(2,1)S(1)}, u32[]{:S(2)}, u32[]{:S(2)}) async-start(bf16[8,16,1024]{2,1,0:T(8,128)(2,1)} %bitcast.45), calls=%async_computation.2 | async-start | bytes 524288 | tf_op jit(solution)/shard_map/all_to_all | solution.py:296
  81.8 4.5 %collective-permute-done.4 = bf16[16,64,128]{2,1,0:T(8,128)(2,1)S(1)} collective-permute-done((bf16[16,64,128]{2,1,0:T(8,128)(2,1)}, bf16[16,64,128]{2,1,0:T(8,128)(2,1)S(1)}, u32[]{:S(2)}, u32[]{:S(2)}) %collective-permute-start.4) | collective-permute-done | bytes 262176 | tf_op jit(solution)/shard_map/ppermute | solution.py:19
  86.3 0.0 collective-permute-done.5
  86.3 0.6 collective-permute-done.6
  86.9 0.9 fusion.2
  87.8 0.1 all-to-all-done.2
  87.9 3.4 %all-to-all-start.1 = ((bf16[8,2,64,128]{3,2,1,0:T(8,128)(2,1)}), bf16[8,2,64,128]{3,2,1,0:T(8,128)(2,1)S(1)}, u32[]{:S(2)}, u32[]{:S(2)}) async-start(bf16[8,2,64,128]{3,2,1,0:T(8,128)(2,1)} %bitcast.18), calls=%async_computation.1 | async-start | bytes 524288 | tf_op jit(solution)/shard_map/all_to_all | solution.py:281
  91.3 0.7 constant_dynamic-slice_fusion
  92.0 0.7 reduce_sum.35
  92.7 10.3 %all-to-all-done.1 = bf16[8,2,64,128]{3,2,1,0:T(8,128)(2,1)S(1)} async-done(((bf16[8,2,64,128]{3,2,1,0:T(8,128)(2,1)}), bf16[8,2,64,128]{3,2,1,0:T(8,128)(2,1)S(1)}, u32[]{:S(2)}, u32[]{:S(2)}) %all-to-all-start.1) | async-done | bytes 262176 | tf_op jit(solution)/shard_map/all_to_all | solution.py:281
  103.1 0.1 fusion.7
  103.2 0.1 copy.24
  103.3 0.6 copy.23
  103.9 0.1 fusion.8
  104.0 0.6 copy.22
  (5 shorter events, 0.1 us)
Async XLA Ops:
  1.5 2.8 %copy-start.8 = (bf16[1024,16,192]{0,2,1:T(8,128)(2,1)S(1)}, bf16[1024,16,192]{0,2,1:T(8,128)(2,1)}, u32[]{:S(2)}) copy-start(bf16[1024,16,192]{0,2,1:T(8,128)(2,1)} %param.8) | copy-start | bytes 18874372
  4.3 1.9 %copy-start.9 = (bf16[512,16,192]{0,2,1:T(8,128)(2,1)S(1)}, bf16[512,16,192]{0,2,1:T(8,128)(2,1)}, u32[]{:S(2)}) copy-start(bf16[512,16,192]{0,2,1:T(8,128)(2,1)} %param.7) | copy-start | bytes 9437188
  6.2 9.0 %copy-start.10 = (bf16[64,64]{1,0:T(8,128)(2,1)S(1)}, bf16[64,64]{1,0:T(8,128)(2,1)}, u32[]{:S(2)}) copy-start(bf16[64,64]{1,0:T(8,128)(2,1)} %param.11) | copy-start | bytes 24580
  15.1 2.0 %collective-permute-start = (bf16[4,64,1024]{2,1,0:T(8,128)(2,1)S(1)}, bf16[4,64,1024]{2,1,0:T(8,128)(2,1)S(1)}, u32[]{:S(2)}, u32[]{:S(2)}) collective-permute-start(bf16[4,64,1024]{2,1,0:T(8,128)(2,1)S(1)} %get-tuple-element.13), channel_id=1, source_target_pairs={{0,32},{32,0},{1,33},{33,1},{2,34},{34,2},{3,35},{35,3},{4,36},{36... | collective-permute-start | bytes 1572872 | tf_op jit(solution)/shard_map/ppermute | solution.py:19
  17.9 18.7 %collective-permute-start.1 = (bf16[64,1024]{1,0:T(8,128)(2,1)}, bf16[64,1024]{1,0:T(8,128)(2,1)}, u32[]{:S(2)}, u32[]{:S(2)}) collective-permute-start(bf16[64,1024]{1,0:T(8,128)(2,1)} %get-tuple-element.29), channel_id=1, source_target_pairs={{0,64},{64,128},{128,192},{192,0},{1,65},{65,129},{129,193},{193,1... | collective-permute-start | bytes 393224 | tf_op jit(solution)/shard_map/ppermute | solution.py:19
  19.5 17.1 %collective-permute-start.2 = (bf16[64,1024]{1,0:T(8,128)(2,1)}, bf16[64,1024]{1,0:T(8,128)(2,1)}, u32[]{:S(2)}, u32[]{:S(2)}) collective-permute-start(bf16[64,1024]{1,0:T(8,128)(2,1)} %get-tuple-element.28), channel_id=1, source_target_pairs={{0,128},{64,192},{128,0},{192,64},{1,129},{65,193},{129,1},{193,65... | collective-permute-start | bytes 393224 | tf_op jit(solution)/shard_map/ppermute | solution.py:19
  22.2 14.4 %collective-permute-start.3 = (bf16[64,1024]{1,0:T(8,128)(2,1)}, bf16[64,1024]{1,0:T(8,128)(2,1)}, u32[]{:S(2)}, u32[]{:S(2)}) collective-permute-start(bf16[64,1024]{1,0:T(8,128)(2,1)} %get-tuple-element.27), channel_id=1, source_target_pairs={{0,192},{64,0},{128,64},{192,128},{1,193},{65,1},{129,65},{193,129... | collective-permute-start | bytes 393224 | tf_op jit(solution)/shard_map/ppermute | solution.py:19
  24.2 2.0 %copy-start.2 = (bf16[1024,128]{1,0:T(8,128)(2,1)S(1)}, bf16[1024,128]{1,0:T(8,128)(2,1)}, u32[]{:S(2)}) copy-start(bf16[1024,128]{1,0:T(8,128)(2,1)} %keys.3) | copy-start | bytes 786436
  33.3 3.2 %copy-start = (bf16[64,64,1024]{2,1,0:T(8,128)(2,1)}, bf16[64,64,1024]{2,1,0:T(8,128)(2,1)S(1)}, u32[]{:S(2)}) copy-start(bf16[64,64,1024]{2,1,0:T(8,128)(2,1)S(1)} %get-tuple-element.16.mask) | copy-start | bytes 25165828
  36.6 25.5 %copy-start.7 = (f32[64]{0:T(128)S(1)}, f32[64]{0:T(128)}, u32[]{:S(2)}) copy-start(f32[64]{0:T(128)} %param.13) | copy-start | bytes 772
  37.9 0.7 copy-start.4
  39.4 21.4 %all-to-all-start = ((f32[32,1,512]{2,1,0:T(1,128)}), f32[32,1,512]{2,1,0:T(1,128)S(1)}, u32[]{:S(2)}, u32[]{:S(2)}) async-start(f32[32,1,512]{2,1,0:T(1,128)} %reshape.37), calls=%async_computation | async-start | bytes 131072 | tf_op jit(solution)/shard_map/all_to_all | solution.py:269
  62.1 3.4 %copy-start.1 = (bf16[64,64,1024]{2,1,0:T(8,128)(2,1)S(1)}, bf16[64,64,1024]{2,1,0:T(8,128)(2,1)}, u32[]{:S(2)}) copy-start(bf16[64,64,1024]{2,1,0:T(8,128)(2,1)} %copy-done) | copy-start | bytes 25165828
  65.5 0.9 copy-start.3
  66.5 0.9 copy-start.5
  72.2 4.9 %copy-start.6 = (bf16[128,1024]{1,0:T(8,128)(2,1)}, bf16[128,1024]{1,0:T(8,128)(2,1)S(1)}, u32[]{:S(2)}) copy-start(bf16[128,1024]{1,0:T(8,128)(2,1)S(1)} %get-tuple-element.18) | copy-start | bytes 786436
  73.1 13.2 %collective-permute-start.4 = (bf16[16,64,128]{2,1,0:T(8,128)(2,1)}, bf16[16,64,128]{2,1,0:T(8,128)(2,1)S(1)}, u32[]{:S(2)}, u32[]{:S(2)}) collective-permute-start(bf16[16,64,128]{2,1,0:T(8,128)(2,1)} %get-tuple-element.24), channel_id=1, source_target_pairs={{0,8},{8,16},{16,24},{24,0},{1,9},{9,17},{17,25},{25,1},{2,10},{10... | collective-permute-start | bytes 786440 | tf_op jit(solution)/shard_map/ppermute | solution.py:19
  73.8 12.5 %collective-permute-start.5 = (bf16[16,64,128]{2,1,0:T(8,128)(2,1)}, bf16[16,64,128]{2,1,0:T(8,128)(2,1)S(1)}, u32[]{:S(2)}, u32[]{:S(2)}) collective-permute-start(bf16[16,64,128]{2,1,0:T(8,128)(2,1)} %get-tuple-element.26), channel_id=1, source_target_pairs={{0,16},{8,24},{16,0},{24,8},{1,17},{9,25},{17,1},{25,9},{2,18},{10... | collective-permute-start | bytes 786440 | tf_op jit(solution)/shard_map/ppermute | solution.py:19
  75.8 11.1 %collective-permute-start.6 = (bf16[16,64,128]{2,1,0:T(8,128)(2,1)S(1)}, bf16[16,64,128]{2,1,0:T(8,128)(2,1)S(1)}, u32[]{:S(2)}, u32[]{:S(2)}) collective-permute-start(bf16[16,64,128]{2,1,0:T(8,128)(2,1)S(1)} %get-tuple-element.25), channel_id=1, source_target_pairs={{0,24},{8,0},{16,8},{24,16},{1,25},{9,1},{17,9},{25,17},{2,26},{10... | collective-permute-start | bytes 786440 | tf_op jit(solution)/shard_map/ppermute | solution.py:19
  77.1 10.7 %all-to-all-start.2 = ((bf16[8,16,1024]{2,1,0:T(8,128)(2,1)}), bf16[8,16,1024]{2,1,0:T(8,128)(2,1)S(1)}, u32[]{:S(2)}, u32[]{:S(2)}) async-start(bf16[8,16,1024]{2,1,0:T(8,128)(2,1)} %bitcast.45), calls=%async_computation.2 | async-start | bytes 524288 | tf_op jit(solution)/shard_map/all_to_all | solution.py:296
  87.9 15.1 %all-to-all-start.1 = ((bf16[8,2,64,128]{3,2,1,0:T(8,128)(2,1)}), bf16[8,2,64,128]{3,2,1,0:T(8,128)(2,1)S(1)}, u32[]{:S(2)}, u32[]{:S(2)}) async-start(bf16[8,2,64,128]{3,2,1,0:T(8,128)(2,1)} %bitcast.18), calls=%async_computation.1 | async-start | bytes 524288 | tf_op jit(solution)/shard_map/all_to_all | solution.py:281

commit v2 on v1

v2 whole, which is shorter than its diff:
```python
import functools
import math

import jax
import jax.numpy as jnp
from jax import lax
from jax.experimental import pallas as pl
from jax.experimental.pallas import tpu as pltpu
from jax.sharding import Mesh, PartitionSpec as P

F32 = jnp.float32
BF16 = jnp.bfloat16
NY, NC, NX, NZ = 4, 2, 4, 8
MIB = 1 << 20
LARGE = pltpu.CompilerParams(vmem_limit_bytes=60 * MIB)
SMALL = pltpu.CompilerParams(vmem_limit_bytes=12 * MIB)
HERE = pl.BlockSpec(memory_space=pltpu.VMEM)
SCALARS = pl.BlockSpec(memory_space=pltpu.SMEM)
AWAY = pl.BlockSpec(memory_space=pl.ANY)


def rotate(array, axis, shift):
    n = lax.axis_size(axis)
    return lax.ppermute(array, axis, [(i, (i + shift) % n) for i in range(n)])


def score_kernel(
    place, queries_far, keys_far, logs, keep, send, queries, keys, total, arrived, *, rows, scale
):
    heads, depth, cols = queries.shape

    def fetch(head):
        return (
            pltpu.make_async_copy(queries_far.at[head], queries.at[head], arrived.at[0, head]),
            pltpu.make_async_copy(keys_far.at[head], keys.at[head], arrived.at[1, head]),
        )

    for head in range(heads):
        for copy in fetch(head):
            copy.start()
    factor = scale * math.log2(math.e)
    ones = jnp.ones((16, keys.shape[2]), BF16)
    line = lax.broadcasted_iota(jnp.int32, (16, cols), 0)

    total[...] = jnp.zeros_like(total)

    def plain_head(head, carry):
        for copy in fetch(head):
            copy.wait()
        log_row = logs[pl.ds(head, 1), :] * (-1.0 / scale)
        high = log_row.astype(BF16).astype(F32)
        rest = log_row - high
        middle = rest.astype(BF16).astype(F32)
        low = rest - middle
        extra = jnp.where(
            line == 0, high, jnp.where(line == 1, middle, jnp.where(line == 2, low, 0.0))
        ).astype(BF16)
        left = jnp.concatenate([queries[head], extra], axis=0).T
        right = jnp.concatenate([keys[head], ones], axis=0)
        tile = 128
        for at in range(0, cols, tile):
            scores = jnp.dot(left[at : at + tile], right, preferred_element_type=F32)
            total[at : at + tile, :] += jnp.exp2(scores * factor)
        return carry

    lax.fori_loop(0, heads, plain_head, 0)
    y, core = place[0], place[1]
    for r in range(NY):
        base = lax.rem(y + r, NY) * (NC * rows)
        mine = pl.multiple_of(base + core * rows, rows)
        other = pl.multiple_of(base + (1 - core) * rows, rows)
        keep[r] = total[pl.ds(mine, rows), :].astype(BF16)
        send[r] = total[pl.ds(other, rows), :].astype(BF16)


def head_scores(place, queries, keys, logs, rows, scale):
    heads, depth, count = queries.shape
    width = keys.shape[2]
    out = jax.ShapeDtypeStruct((NY, rows, width), BF16)
    return pl.pallas_call(
        functools.partial(score_kernel, rows=rows, scale=scale),
        in_specs=[SCALARS, AWAY, AWAY, HERE],
        out_specs=[HERE, HERE],
        scratch_shapes=[
            pltpu.VMEM(queries.shape, BF16),
            pltpu.VMEM(keys.shape, BF16),
            pltpu.VMEM((count, width), F32),
            pltpu.SemaphoreType.DMA((2, heads)),
        ],
        out_shape=[out, out],
        compiler_params=LARGE,
        cost_estimate=pl.CostEstimate(
            flops=2 * heads * depth * count * width,
            bytes_accessed=12 * MIB,
            transcendentals=heads * count * width,
        ),
        name="head_scores",
    )(place, queries, keys, logs)


def column(array, index):
    lane = lax.broadcasted_iota(jnp.int32, array.shape, 1)
    return jnp.sum(jnp.where(lane == index, array, 0.0), axis=1, keepdims=True)


def logit_kernel(queries, keys, weights, expo, sums, mask, scaled, logits):
    heads, rows, depth = queries.shape
    width = keys.shape[0]
    group, tile = 8, 256
    every = weights[...].astype(F32)
    logits[...] = jnp.zeros_like(logits)

    def some_heads(step, carry):
        first = step * group
        columns = [column(every, first + k) for k in range(group)]
        here = queries[pl.ds(first, group)]
        for k in range(group):
            scaled[first + k] = (here[k].astype(F32) * columns[k]).astype(BF16)
        flat = here.reshape(group * rows, depth)
        for at in range(0, width, tile):
            raw = lax.dot_general(
                flat, keys[at : at + tile], (((1,), (1,)), ((), ())), preferred_element_type=F32
            ).reshape(group, rows, tile)
            mask[pl.ds(first, group), :, at : at + tile] = jnp.where(raw > 0, 1.0, 0.0).astype(BF16)
            added = logits[:, at : at + tile]
            for k in range(group):
                added += columns[k] * jnp.maximum(raw[k], 0.0)
            logits[:, at : at + tile] = added
        return carry

    lax.fori_loop(0, heads // group, some_heads, 0)
    values = logits[...]
    top = jnp.max(values, axis=1, keepdims=True)
    powers = jnp.exp(values - top)
    total = jnp.sum(powers, axis=1, keepdims=True)
    lane = lax.broadcasted_iota(jnp.int32, sums.shape, 1)
    expo[...] = powers
    sums[...] = jnp.where(lane == 0, top, jnp.where(lane == 1, total, 0.0))


def index_logits(queries, keys, weights):
    heads, rows, depth = queries.shape
    width = keys.shape[0]
    return pl.pallas_call(
        logit_kernel,
        in_specs=[HERE] * 3,
        out_specs=[HERE] * 4,
        out_shape=[
            jax.ShapeDtypeStruct((rows, width), F32),
            jax.ShapeDtypeStruct((rows, 128), F32),
            jax.ShapeDtypeStruct((heads, rows, width), BF16),
            jax.ShapeDtypeStruct((heads, rows, depth), BF16),
        ],
        scratch_shapes=[pltpu.VMEM((rows, width), F32)],
        compiler_params=SMALL,
        cost_estimate=pl.CostEstimate(
            flops=2 * heads * rows * depth * width,
            bytes_accessed=10 * MIB,
            transcendentals=0,
        ),
        name="index_logits",
    )(queries, keys, weights)


def stats_kernel(sums, one, two, three, four, probs, stats):
    summed = (
        one[...].astype(F32) + two[...].astype(F32) + three[...].astype(F32) + four[...].astype(F32)
    )
    probs[...] = summed
    mass = jnp.sum(summed, axis=1, keepdims=True)
    lane = lax.broadcasted_iota(jnp.int32, sums.shape, 1)
    packed = jnp.where(lane == 2, mass, sums[...])
    line = packed.T[:8]
    full = jnp.concatenate([line, jnp.zeros_like(line)], axis=1)
    stats[...] = jnp.broadcast_to(full[None], stats.shape)


def local_stats(sums, parts):
    rows, width = parts[0].shape
    return pl.pallas_call(
        stats_kernel,
        out_shape=[
            jax.ShapeDtypeStruct((rows, width), F32),
            jax.ShapeDtypeStruct((NX * NZ, 8, 2 * rows), F32),
        ],
        in_specs=[HERE] * (1 + len(parts)),
        out_specs=[HERE, HERE],
        compiler_params=SMALL,
        name="local_stats",
    )(sums, *parts)


def query_terms(mask, first, keys, values, out):
    count, rows, depth = out.shape
    width = keys.shape[0]
    half = count // 2
    for at in range(0, count, half):
        gated = (mask[pl.ds(first + at, half)] * values[None]).reshape(half * rows, width)
        term = jnp.dot(gated, keys[...], preferred_element_type=F32)
        out[at : at + half] = term.astype(BF16).reshape(half, rows, depth)


def far_kernel(place, expo, sums, probs, stats, loss, mask, keys, grads, one, two, three):
    rows = expo.shape[0]
    each = stats[...]
    tops = each[:, 0, :]
    top = jnp.max(tops, axis=0, keepdims=True)
    denominator = jnp.sum(each[:, 1, :] * jnp.exp(tops - top), axis=0, keepdims=True)
    mass = jnp.sum(each[:, 2, :], axis=0, keepdims=True)
    line = lax.broadcasted_iota(jnp.int32, (128, 2 * rows), 0)
    packed = jnp.where(line == 0, top, jnp.where(line == 1, denominator, mass)).T[:rows]
    weight = jnp.broadcast_to(loss[...], (128, rows)).T[:, 0:1]
    soft = expo[...] * (jnp.exp(sums[:, 0:1] - packed[:, 0:1]) / packed[:, 1:2])
    target = probs[...] / packed[:, 2:3]
    values = (weight * (soft - target)).astype(BF16)
    grads[...] = values
    for r, out in ((1, one), (2, two), (3, three)):
        first = lax.rem(place[2] + r, NX) * out.shape[0]
        query_terms(mask, first, keys, values, out)


def far_terms(place, expo, sums, probs, stats, loss, mask, keys):
    heads, rows, width = mask.shape
    depth = keys.shape[1]
    part = jax.ShapeDtypeStruct((heads // NX, rows, depth), BF16)
    return pl.pallas_call(
        far_kernel,
        in_specs=[SCALARS] + [HERE] * 7,
        out_specs=[HERE] * 4,
        out_shape=[jax.ShapeDtypeStruct((rows, width), BF16), part, part, part],
        compiler_params=SMALL,
        cost_estimate=pl.CostEstimate(
            flops=heads * rows * depth * width, bytes_accessed=8 * MIB, transcendentals=0
        ),
        name="far_terms",
    )(place, expo, sums, probs, stats, loss, mask, keys)


def near_kernel(place, grads, mask, keys, scaled, own, key_part, total):
    heads, rows, width = mask.shape
    depth = keys.shape[1]
    values = grads[...]
    query_terms(mask, place[2] * own.shape[0], keys, values, own)
    group = 8
    total[...] = jnp.zeros_like(total)

    def some_heads(step, carry):
        first = step * group
        gated = (mask[pl.ds(first, group)] * values[None]).reshape(group * rows, width)
        left = scaled[pl.ds(first, group)].reshape(group * rows, depth)
        total[...] += lax.dot_general(
            left, gated, (((0,), (0,)), ((), ())), preferred_element_type=F32
        )
        return carry

    lax.fori_loop(0, heads // group, some_heads, 0)
    key_part[...] = total[...].astype(BF16)


def near_terms(place, grads, mask, keys, scaled):
    heads, rows, width = mask.shape
    depth = keys.shape[1]
    return pl.pallas_call(
        near_kernel,
        in_specs=[SCALARS] + [HERE] * 4,
        out_specs=[HERE] * 2,
        scratch_shapes=[pltpu.VMEM((depth, width), F32)],
        out_shape=[
            jax.ShapeDtypeStruct((heads // NX, rows, depth), BF16),
            jax.ShapeDtypeStruct((depth, width), BF16),
        ],
        compiler_params=SMALL,
        cost_estimate=pl.CostEstimate(
            flops=3 * heads * rows * depth * width, bytes_accessed=10 * MIB, transcendentals=0
        ),
        name="near_terms",
    )(place, grads, mask, keys, scaled)


def last_kernel(place, pieces, queries, weights, query_grad, weight_grad):
    summed = pieces[0].astype(F32)
    for k in range(1, pieces.shape[0]):
        summed += pieces[k].astype(F32)
    mine = pieces.shape[1]
    every = weights[...].astype(F32)
    for k in range(mine):
        dots = jnp.sum(summed[k] * queries[k].astype(F32), axis=1, keepdims=True)
        weight_grad[k : k + 1, :] = jnp.broadcast_to(dots, (dots.shape[0], 128)).T[0:1]
        query_grad[:, k, :] = (summed[k] * column(every, place[3] * mine + k)).astype(BF16)


def last_sums(place, pieces, queries, weights):
    count, mine, rows, depth = pieces.shape
    return pl.pallas_call(
        last_kernel,
        grid_spec=pltpu.PrefetchScalarGridSpec(
            num_scalar_prefetch=1,
            grid=(1,),
            in_specs=[
                pl.BlockSpec(pieces.shape, lambda i, p: (0, 0, 0, 0)),
                pl.BlockSpec((mine, rows, depth), lambda i, p: (p[3], 0, 0)),
                pl.BlockSpec(weights.shape, lambda i, p: (0, 0)),
            ],
            out_specs=[
                pl.BlockSpec((rows, mine, depth), lambda i, p: (0, 0, 0)),
                pl.BlockSpec((mine, rows), lambda i, p: (0, 0)),
            ],
        ),
        out_shape=[
            jax.ShapeDtypeStruct((rows, mine, depth), BF16),
            jax.ShapeDtypeStruct((mine, rows), F32),
        ],
        compiler_params=SMALL,
        name="last_sums",
    )(place, pieces, queries, weights)


def per_device(
    main_queries, main_keys, log_sums, index_queries, index_weights, index_keys, loss_weights
):
    rows, heads, depth = index_queries.shape
    width = index_keys.shape[0]
    scale = main_queries.shape[2] ** (-0.5)
    x, z = lax.axis_index("x"), lax.axis_index("z")
    place = jnp.stack([lax.axis_index("y"), lax.axis_index("core"), x, x * NZ + z])

    keep, send = head_scores(
        place,
        jnp.transpose(main_queries, (1, 2, 0)),
        jnp.transpose(main_keys, (1, 2, 0)),
        log_sums.T,
        rows,
        scale,
    )
    arrived = rotate(send, "core", 1)
    pairs = [(keep[r].astype(F32) + arrived[r].astype(F32)).astype(BF16) for r in range(NY)]
    parts = [pairs[0]] + [rotate(pairs[r], "y", r) for r in range(1, NY)]

    turned = jnp.transpose(index_queries, (1, 0, 2))
    expo, sums, mask, scaled = index_logits(turned, index_keys, index_weights)

    probs, stats = local_stats(sums, parts)
    everywhere = lax.all_to_all(stats, ("x", "z"), split_axis=0, concat_axis=0, tiled=True)
    grads, one, two, three = far_terms(
        place, expo, sums, probs, everywhere, loss_weights[None], mask, index_keys
    )
    across = [rotate(term, "x", r) for r, term in ((1, one), (2, two), (3, three))]
    own, key_part = near_terms(place, grads, mask, index_keys, scaled)
    summed = sum(part.astype(F32) for part in [own] + across).astype(BF16)
    pieces = lax.all_to_all(
        summed.reshape(NZ, heads // (NX * NZ), rows, depth),
        "z",
        split_axis=0,
        concat_axis=0,
        tiled=True,
    )
    query_grad, weight_grad = last_sums(place, pieces, turned, index_weights)

    key_pieces = lax.all_to_all(
        key_part.reshape(NY * NC, depth // (NY * NC), width),
        ("y", "core"),
        split_axis=0,
        concat_axis=0,
        tiled=True,
    )
    key_grad = key_pieces.astype(F32).sum(axis=0).astype(BF16).T
    return query_grad, weight_grad.T, key_grad


def solution(mesh):
    fine = Mesh(mesh.devices.reshape(NY, NC, NX, NZ), ("y", "core", "x", "z"))
    head, ctx = ("y", "core"), ("x", "z")
    return jax.shard_map(
        per_device,
        mesh=fine,
        in_specs=(
            P(None, head, None),
            P(ctx, head, None),
            P(None, head),
            P(head, None, None),
            P(head, None),
            P(ctx, None),
            P(head),
        ),
        out_specs=(P(head, ctx, None), P(head, ctx), P(ctx, head)),
        check_vma=False,
    )
```

time: 106 us -> 88.8 us (0.84)
  blocking collectives: 0 us -> 21.5 us
  local copies, waits for them, and re-layouts: 21.7 us -> 0.7 us
  starting transfers between devices: 28.5 us -> 18.6 us
  waiting for transfers between devices: 25.5 us -> 18.4 us
  Pallas kernels: 22.2 us -> 24.9 us
  other arithmetic: 5.93 us -> 3.45 us
    all_to_all x0 -> x1, blocking collectives: none -> 21.5 us  [per_device(): lax.all_to_all(stats, ('x', 'z'), split_axis=0, concat_axis=0, tiled=True)]
    unnamed x29 -> x11, local copies, waits for them, and re-layouts: 18.2 us -> 0.7 us
    all_to_all x1 -> x0, starting transfers between devices: 11.4 us -> none  [per_device(): lax.all_to_all(jnp.broadcast_to(stats[None], (NX * NZ, *stats.shape)), ('...]
    all_to_all x1 -> x0, waiting for transfers between devices: 8.17 us -> none  [per_device(): lax.all_to_all(jnp.broadcast_to(stats[None], (NX * NZ, *stats.shape)), ('...]
    all_to_all x1, waiting for transfers between devices: 0.09 us -> 5.2 us  [per_device(): lax.all_to_all(key_part.reshape(NY * NC, depth // (NY * NC), width), ('y'...]
    ppermute x7, waiting for transfers between devices: 6.92 us -> 2.12 us  [rotate(): return lax.ppermute(array, axis, [(i, (i + shift) % n) for i in range(n)])]
    pallas_call x3 -> x5, Pallas kernels: 20.9 us -> 24.7 us  [the longest x1 11.3 us: head_scores(): pl.pallas_call(functools.partial(score_kernel, rows=rows, scale=scale), i...]
    convert_element_type x4 -> x1, other arithmetic: 3.39 us -> 0.87 us  [per_device(): summed = sum((part.astype(F32) for part in [own] + across)).astype(BF16)]
  transfers between devices with their start and end apart: 10 -> 9, of which waited for: 6 -> 3; matrix products, arithmetic and copies ran while one was open for 7% -> 2% of each run, Pallas kernels for 7% -> 11%
where the time goes in v2:
time: 88.8 us; the launch traced here: 88.3 us
  Pallas kernels  24.9 us (28%)
  blocking collectives  21.5 us (24%)
  starting transfers between devices  18.6 us (21%)
  waiting for transfers between devices  18.4 us (21%)
  other arithmetic  3.45 us (4%)
    all_to_all x1, blocking collectives, per_device(): lax.all_to_all(stats, ('x', 'z'), split_axis=0, concat_axis=0, tiled=True)  21.5 us
    pallas_call x1, Pallas kernels, head_scores(): pl.pallas_call(functools.partial(score_kernel, rows=rows, scale=scale), i...  11.3 us
    all_to_all x1, waiting for transfers between devices, per_device(): lax.all_to_all(summed.reshape(NZ, heads // (NX * NZ), rows, depth), 'z',...  11 us
    ppermute x7, starting transfers between devices, rotate(): return lax.ppermute(array, axis, [(i, (i + shift) % n) for i in range(n)])  9.16 us
    all_to_all x1, starting transfers between devices, per_device(): lax.all_to_all(key_part.reshape(NY * NC, depth // (NY * NC), width), ('y'...  6.02 us
    all_to_all x1, waiting for transfers between devices, per_device(): lax.all_to_all(key_part.reshape(NY * NC, depth // (NY * NC), width), ('y'...  5.2 us
    pallas_call x1, Pallas kernels, near_terms(): pl.pallas_call(near_kernel, in_specs=[SCALARS] + [HERE] * 4, out_specs=[H...  4.72 us
    pallas_call x1, Pallas kernels, index_logits(): pl.pallas_call(logit_kernel, in_specs=[HERE] * 3, out_specs=[HERE] * 4, o...  4.72 us
  transfers between devices with their start and end apart: 9, of which 3 were waited for; matrix products, arithmetic and copies ran while one was open for 2% of the time, Pallas kernels for 11%

profile of v2, /device:TPU:8, one launch (start us, length us, event | category | flops | bytes accessed | tf_op | source)
XLA Modules:
  0.0 88.3 jit_solution(8333636116877360503)
XLA Ops:
  0.6 0.7 pad_add_fusion.place
  1.3 0.0 copy-start.4
  1.3 0.0 copy-start
  1.3 0.0 copy-start.1
  1.3 11.3 %head_scores.1 = (bf16[4,64,1024]{2,1,0:T(8,128)(2,1)}, bf16[4,64,1024]{2,1,0:T(8,128)(2,1)}) custom-call(s32[4]{0:T(128)} %pad_add_fusion.place, bf16[16,192,512]{2,1,0:T(8,128)(2,1)} %bitcast.28, bf16[16,192,1024]{2,1,0:T(8,128)(2,1)} %bitcast.27, f32[16,512]{1,0:T(8,128)} %bitcast.29), custom_call_target="tpu_custom_call" | custom-call | flops 3221225472 | bytes 12582912 | tf_op jit(solution)/shard_map/head_scores/pallas_call | solution.py:80
  12.6 0.0 copy-start.2
  12.6 0.0 copy-start.3
  12.6 0.1 collective-permute-start
  12.7 2.1 %collective-permute-done = bf16[4,64,1024]{2,1,0:T(8,128)(2,1)S(1)} collective-permute-done((bf16[4,64,1024]{2,1,0:T(8,128)(2,1)}, bf16[4,64,1024]{2,1,0:T(8,128)(2,1)S(1)}, u32[]{:S(2)}, u32[]{:S(2)}) %collective-permute-start) | collective-permute-done | bytes 524320 | tf_op jit(solution)/shard_map/ppermute | solution.py:24
  14.8 1.3 %fusion.3 = (bf16[64,1024]{1,0:T(8,128)(2,1)S(1)}, bf16[64,1024]{1,0:T(8,128)(2,1)S(1)}, bf16[64,1024]{1,0:T(8,128)(2,1)S(1)}, bf16[64,1024]{1,0:T(8,128)(2,1)S(1)}) fusion(bf16[4,64,1024]{2,1,0:T(8,128)(2,1)S(1)} %collective-permute-done, bf16[4,64,1024]{2,1,0:T(8,128)(2,1)} %get-tuple-element.21), kind=kLoop, calls=%fused_computation.9 | loop fusion | flops 1048576 | bytes 1572864 | tf_op jit(solution)/shard_map/convert_element_type | solution.py:336
  16.1 2.2 %collective-permute-start.3 = (bf16[64,1024]{1,0:T(8,128)(2,1)S(1)}, bf16[64,1024]{1,0:T(8,128)(2,1)S(1)}, u32[]{:S(2)}, u32[]{:S(2)}) collective-permute-start(bf16[64,1024]{1,0:T(8,128)(2,1)S(1)} %get-tuple-element.35), channel_id=1, source_target_pairs={{0,192},{64,0},{128,64},{192,128},{1,193},{65,1},{129,65},{193,129... | collective-permute-start | bytes 393224 | tf_op jit(solution)/shard_map/ppermute | solution.py:24
  18.3 0.9 collective-permute-start.2
  19.2 1.9 %collective-permute-start.1 = (bf16[64,1024]{1,0:T(8,128)(2,1)S(1)}, bf16[64,1024]{1,0:T(8,128)(2,1)S(1)}, u32[]{:S(2)}, u32[]{:S(2)}) collective-permute-start(bf16[64,1024]{1,0:T(8,128)(2,1)S(1)} %get-tuple-element.37), channel_id=1, source_target_pairs={{0,64},{64,128},{128,192},{192,0},{1,65},{65,129},{129,193},{193,1... | collective-permute-start | bytes 393224 | tf_op jit(solution)/shard_map/ppermute | solution.py:24
  21.1 0.0 copy-done.4
  21.1 0.7 copy.12
  21.8 0.0 copy-done
  21.8 0.0 copy-done.1
  21.8 4.7 %index_logits.1 = (f32[64,1024]{1,0:T(8,128)S(1)}, f32[64,128]{1,0:T(8,128)S(1)}, bf16[64,64,1024]{2,1,0:T(8,128)(2,1)S(1)}, bf16[64,64,128]{2,1,0:T(8,128)(2,1)S(1)}) custom-call(bf16[64,64,128]{2,1,0:T(8,128)(2,1)S(1)} %bitcast.23, bf16[1024,128]{1,0:T(8,128)(2,1)S(1)} %copy-done, bf16[64,64]{1,0:T(8,128)(2,1)S(1)} %copy-done.1), custom_call_target="tpu_custom_call" | custom-call | flops 1073741824 | bytes 10485760 | tf_op jit(solution)/shard_map/index_logits/pallas_call | solution.py:144
  26.5 0.0 collective-permute-done.3.four
  26.6 0.0 collective-permute-done.2.three
  26.6 0.0 collective-permute-done.1.two
  26.6 0.2 local_stats.1
  26.8 21.5 %all_to_all.15.stats = f32[32,8,128]{2,1,0:T(8,128)S(1)} all-to-all(f32[32,8,128]{2,1,0:T(8,128)S(1)} %get-tuple-element.24), channel_id=1, replica_groups=mesh['y'=4,'core'=2,'x'=4,'z'=8] {'x','z'}, dimensions={0} | all-to-all | bytes 262144 | tf_op jit(solution)/shard_map/all_to_all | solution.py:343
  48.3 0.0 copy-done.2
  48.3 0.0 copy-done.3
  48.3 2.6 %far_terms.1 = (bf16[64,1024]{1,0:T(8,128)(2,1)S(1)}, bf16[16,64,128]{2,1,0:T(8,128)(2,1)S(1)}, bf16[16,64,128]{2,1,0:T(8,128)(2,1)S(1)}, bf16[16,64,128]{2,1,0:T(8,128)(2,1)S(1)}) custom-call(s32[4]{0:T(128)S(1)} %copy-done.2, f32[64,1024]{1,0:T(8,128)S(1)} %get-tuple-element.19.expo, f32[64,128]{1,0:T(8,128)S(1)} %get-tuple-element.20.sums, ...), custom_call_target="tpu_custom_call" | custom-call | flops 536870912 | bytes 8388608 | tf_op jit(solution)/shard_map/far_terms/pallas_call | solution.py:226
  50.9 0.7 collective-permute-start.4
  51.6 2.1 %collective-permute-start.5 = (bf16[16,64,128]{2,1,0:T(8,128)(2,1)S(1)}, bf16[16,64,128]{2,1,0:T(8,128)(2,1)S(1)}, u32[]{:S(2)}, u32[]{:S(2)}) collective-permute-start(bf16[16,64,128]{2,1,0:T(8,128)(2,1)S(1)} %get-tuple-element.30), channel_id=1, source_target_pairs={{0,16},{8,24},{16,0},{24,8},{1,17},{9,25},{17,1},{25,9},{2,18},{10... | collective-permute-start | bytes 786440 | tf_op jit(solution)/shard_map/ppermute | solution.py:24
  53.7 1.3 %collective-permute-start.6 = (bf16[16,64,128]{2,1,0:T(8,128)(2,1)S(1)}, bf16[16,64,128]{2,1,0:T(8,128)(2,1)S(1)}, u32[]{:S(2)}, u32[]{:S(2)}) collective-permute-start(bf16[16,64,128]{2,1,0:T(8,128)(2,1)S(1)} %get-tuple-element.31), channel_id=1, source_target_pairs={{0,24},{8,0},{16,8},{24,16},{1,25},{9,1},{17,9},{25,17},{2,26},{10... | collective-permute-start | bytes 786440 | tf_op jit(solution)/shard_map/ppermute | solution.py:24
  55.0 4.7 %near_terms.1 = (bf16[16,64,128]{2,1,0:T(8,128)(2,1)S(1)}, bf16[128,1024]{1,0:T(8,128)(2,1)}) custom-call(s32[4]{0:T(128)S(1)} %copy-done.2, bf16[64,1024]{1,0:T(8,128)(2,1)S(1)} %get-tuple-element.26.grads, bf16[64,64,1024]{2,1,0:T(8,128)(2,1)S(1)} %get-tuple-element.25.mask, bf16[1024,128]{1,0:T(8,128)(2,1)S(1)} %copy-done, ...), custom_call_target="tpu_custom_call" | custom-call | flops 1610612736 | bytes 10485760 | tf_op jit(solution)/shard_map/near_terms/pallas_call | solution.py:263
  59.7 6.0 %all-to-all-start.2 = ((bf16[8,16,1024]{2,1,0:T(8,128)(2,1)}), bf16[8,16,1024]{2,1,0:T(8,128)(2,1)S(1)}, u32[]{:S(2)}, u32[]{:S(2)}) async-start(bf16[8,16,1024]{2,1,0:T(8,128)(2,1)} %bitcast.15), calls=%async_computation.2 | async-start | bytes 524288 | tf_op jit(solution)/shard_map/all_to_all | solution.py:359
  65.7 0.0 collective-permute-done.4
  65.7 0.0 collective-permute-done.5
  65.7 0.0 collective-permute-done.6
  65.8 0.9 add_convert_fusion
  66.6 5.2 %all-to-all-done.2 = bf16[8,16,1024]{2,1,0:T(8,128)(2,1)S(1)} async-done(((bf16[8,16,1024]{2,1,0:T(8,128)(2,1)}), bf16[8,16,1024]{2,1,0:T(8,128)(2,1)S(1)}, u32[]{:S(2)}, u32[]{:S(2)}) %all-to-all-start.2) | async-done | bytes 262176 | tf_op jit(solution)/shard_map/all_to_all | solution.py:359
  71.8 3.4 %all-to-all-start.1 = ((bf16[8,2,64,128]{3,2,1,0:T(8,128)(2,1)}), bf16[8,2,64,128]{3,2,1,0:T(8,128)(2,1)S(1)}, u32[]{:S(2)}, u32[]{:S(2)}) async-start(bf16[8,2,64,128]{3,2,1,0:T(8,128)(2,1)} %bitcast.13), calls=%async_computation.1 | async-start | bytes 524288 | tf_op jit(solution)/shard_map/all_to_all | solution.py:350
  75.2 0.7 reduce_sum.12
  75.9 11.0 %all-to-all-done.1.pieces = bf16[8,2,64,128]{3,2,1,0:T(8,128)(2,1)S(1)} async-done(((bf16[8,2,64,128]{3,2,1,0:T(8,128)(2,1)}), bf16[8,2,64,128]{3,2,1,0:T(8,128)(2,1)S(1)}, u32[]{:S(2)}, u32[]{:S(2)}) %all-to-all-start.1) | async-done | bytes 262176 | tf_op jit(solution)/shard_map/all_to_all | solution.py:350
  86.9 1.4 %last_sums.1 = (bf16[64,2,128]{2,1,0:T(2,128)(2,1)}, f32[2,64]{1,0:T(2,128)}) custom-call(s32[4]{0:T(128)S(1)} %copy-done.2, bf16[8,2,64,128]{3,2,1,0:T(8,128)(2,1)S(1)} %all-to-all-done.1.pieces, bf16[64,64,128]{2,1,0:T(8,128)(2,1)S(1)} %bitcast.24, bf16[64,64]{1,0:T(8,128)(2,1)S(1)} %copy-done.1), custom_call_target="tpu_custom_call" | custom-call | tf_op jit(solution)/shard_map/last_sums/pallas_call | solution.py:294
Async XLA Ops:
  1.3 19.8 %copy-start.4 = (bf16[64,64,128]{2,1,0:T(8,128)(2,1)S(1)}, bf16[64,64,128]{2,1,0:T(8,128)(2,1)}, u32[]{:S(2)}) copy-start(bf16[64,64,128]{2,1,0:T(8,128)(2,1)} %param.10) | copy-start | bytes 3145732
  1.3 20.5 %copy-start = (bf16[1024,128]{1,0:T(8,128)(2,1)S(1)}, bf16[1024,128]{1,0:T(8,128)(2,1)}, u32[]{:S(2)}) copy-start(bf16[1024,128]{1,0:T(8,128)(2,1)} %keys.5) | copy-start | bytes 786436
  1.3 20.5 %copy-start.1 = (bf16[64,64]{1,0:T(8,128)(2,1)S(1)}, bf16[64,64]{1,0:T(8,128)(2,1)}, u32[]{:S(2)}) copy-start(bf16[64,64]{1,0:T(8,128)(2,1)} %weights.3) | copy-start | bytes 24580
  12.6 35.7 %copy-start.2 = (s32[4]{0:T(128)S(1)}, s32[4]{0:T(128)}, u32[]{:S(2)}) copy-start(s32[4]{0:T(128)} %pad_add_fusion.place) | copy-start | bytes 52
  12.6 35.7 %copy-start.3 = (f32[64]{0:T(128)S(1)}, f32[64]{0:T(128)}, u32[]{:S(2)}) copy-start(f32[64]{0:T(128)} %param.13) | copy-start | bytes 772
  12.6 2.2 %collective-permute-start = (bf16[4,64,1024]{2,1,0:T(8,128)(2,1)}, bf16[4,64,1024]{2,1,0:T(8,128)(2,1)S(1)}, u32[]{:S(2)}, u32[]{:S(2)}) collective-permute-start(bf16[4,64,1024]{2,1,0:T(8,128)(2,1)} %get-tuple-element.22), channel_id=1, source_target_pairs={{0,32},{32,0},{1,33},{33,1},{2,34},{34,2},{3,35},{35,3},{4,36},{36... | collective-permute-start | bytes 1572872 | tf_op jit(solution)/shard_map/ppermute | solution.py:24
  16.1 10.4 %collective-permute-start.3 = (bf16[64,1024]{1,0:T(8,128)(2,1)S(1)}, bf16[64,1024]{1,0:T(8,128)(2,1)S(1)}, u32[]{:S(2)}, u32[]{:S(2)}) collective-permute-start(bf16[64,1024]{1,0:T(8,128)(2,1)S(1)} %get-tuple-element.35), channel_id=1, source_target_pairs={{0,192},{64,0},{128,64},{192,128},{1,193},{65,1},{129,65},{193,129... | collective-permute-start | bytes 393224 | tf_op jit(solution)/shard_map/ppermute | solution.py:24
  18.3 8.2 %collective-permute-start.2 = (bf16[64,1024]{1,0:T(8,128)(2,1)S(1)}, bf16[64,1024]{1,0:T(8,128)(2,1)S(1)}, u32[]{:S(2)}, u32[]{:S(2)}) collective-permute-start(bf16[64,1024]{1,0:T(8,128)(2,1)S(1)} %get-tuple-element.36), channel_id=1, source_target_pairs={{0,128},{64,192},{128,0},{192,64},{1,129},{65,193},{129,1},{193,65... | collective-permute-start | bytes 393224 | tf_op jit(solution)/shard_map/ppermute | solution.py:24
  19.2 7.3 %collective-permute-start.1 = (bf16[64,1024]{1,0:T(8,128)(2,1)S(1)}, bf16[64,1024]{1,0:T(8,128)(2,1)S(1)}, u32[]{:S(2)}, u32[]{:S(2)}) collective-permute-start(bf16[64,1024]{1,0:T(8,128)(2,1)S(1)} %get-tuple-element.37), channel_id=1, source_target_pairs={{0,64},{64,128},{128,192},{192,0},{1,65},{65,129},{129,193},{193,1... | collective-permute-start | bytes 393224 | tf_op jit(solution)/shard_map/ppermute | solution.py:24
  50.9 14.8 %collective-permute-start.4 = (bf16[16,64,128]{2,1,0:T(8,128)(2,1)S(1)}, bf16[16,64,128]{2,1,0:T(8,128)(2,1)S(1)}, u32[]{:S(2)}, u32[]{:S(2)}) collective-permute-start(bf16[16,64,128]{2,1,0:T(8,128)(2,1)S(1)} %get-tuple-element.29), channel_id=1, source_target_pairs={{0,8},{8,16},{16,24},{24,0},{1,9},{9,17},{17,25},{25,1},{2,10},{10... | collective-permute-start | bytes 786440 | tf_op jit(solution)/shard_map/ppermute | solution.py:24
  51.6 14.1 %collective-permute-start.5 = (bf16[16,64,128]{2,1,0:T(8,128)(2,1)S(1)}, bf16[16,64,128]{2,1,0:T(8,128)(2,1)S(1)}, u32[]{:S(2)}, u32[]{:S(2)}) collective-permute-start(bf16[16,64,128]{2,1,0:T(8,128)(2,1)S(1)} %get-tuple-element.30), channel_id=1, source_target_pairs={{0,16},{8,24},{16,0},{24,8},{1,17},{9,25},{17,1},{25,9},{2,18},{10... | collective-permute-start | bytes 786440 | tf_op jit(solution)/shard_map/ppermute | solution.py:24
  53.7 12.1 %collective-permute-start.6 = (bf16[16,64,128]{2,1,0:T(8,128)(2,1)S(1)}, bf16[16,64,128]{2,1,0:T(8,128)(2,1)S(1)}, u32[]{:S(2)}, u32[]{:S(2)}) collective-permute-start(bf16[16,64,128]{2,1,0:T(8,128)(2,1)S(1)} %get-tuple-element.31), channel_id=1, source_target_pairs={{0,24},{8,0},{16,8},{24,16},{1,25},{9,1},{17,9},{25,17},{2,26},{10... | collective-permute-start | bytes 786440 | tf_op jit(solution)/shard_map/ppermute | solution.py:24
  59.7 12.1 %all-to-all-start.2 = ((bf16[8,16,1024]{2,1,0:T(8,128)(2,1)}), bf16[8,16,1024]{2,1,0:T(8,128)(2,1)S(1)}, u32[]{:S(2)}, u32[]{:S(2)}) async-start(bf16[8,16,1024]{2,1,0:T(8,128)(2,1)} %bitcast.15), calls=%async_computation.2 | async-start | bytes 524288 | tf_op jit(solution)/shard_map/all_to_all | solution.py:359
  71.8 15.1 %all-to-all-start.1 = ((bf16[8,2,64,128]{3,2,1,0:T(8,128)(2,1)}), bf16[8,2,64,128]{3,2,1,0:T(8,128)(2,1)S(1)}, u32[]{:S(2)}, u32[]{:S(2)}) async-start(bf16[8,2,64,128]{3,2,1,0:T(8,128)(2,1)} %bitcast.13), calls=%async_computation.1 | async-start | bytes 524288 | tf_op jit(solution)/shard_map/all_to_all | solution.py:350

commit v3 on v2

--- a/solution.py
+++ b/solution.py
@@ -12,10 +12,9 @@
 BF16 = jnp.bfloat16
 NY, NC, NX, NZ = 4, 2, 4, 8
 MIB = 1 << 20
-LARGE = pltpu.CompilerParams(vmem_limit_bytes=60 * MIB)
+LARGE = pltpu.CompilerParams(vmem_limit_bytes=50 * MIB)
 SMALL = pltpu.CompilerParams(vmem_limit_bytes=12 * MIB)
 HERE = pl.BlockSpec(memory_space=pltpu.VMEM)
-SCALARS = pl.BlockSpec(memory_space=pltpu.SMEM)
 AWAY = pl.BlockSpec(memory_space=pl.ANY)
 
 
@@ -25,7 +24,7 @@
 
 
 def score_kernel(
-    place, queries_far, keys_far, logs, keep, send, queries, keys, total, arrived, *, rows, scale
+    queries_far, keys_far, logs, keep, send, queries, keys, total, arrived, *, rows, scale
 ):
     heads, depth, cols = queries.shape
 
@@ -42,11 +41,10 @@
     ones = jnp.ones((16, keys.shape[2]), BF16)
     line = lax.broadcasted_iota(jnp.int32, (16, cols), 0)
 
+    tile = 256
     total[...] = jnp.zeros_like(total)
 
-    def plain_head(head, carry):
-        for copy in fetch(head):
-            copy.wait()
+    def operands(head):
         log_row = logs[pl.ds(head, 1), :] * (-1.0 / scale)
         high = log_row.astype(BF16).astype(F32)
         rest = log_row - high
@@ -56,15 +54,26 @@
             line == 0, high, jnp.where(line == 1, middle, jnp.where(line == 2, low, 0.0))
         ).astype(BF16)
         left = jnp.concatenate([queries[head], extra], axis=0).T
-        right = jnp.concatenate([keys[head], ones], axis=0)
-        tile = 128
-        for at in range(0, cols, tile):
-            scores = jnp.dot(left[at : at + tile], right, preferred_element_type=F32)
-            total[at : at + tile, :] += jnp.exp2(scores * factor)
+        return left, jnp.concatenate([keys[head], ones], axis=0)
+
+    group = 4
+
+    def some_heads(step, carry):
+        first = step * group
+        for k in range(group):
+            for copy in fetch(first + k):
+                copy.wait()
+        pairs = [operands(first + k) for k in range(group)]
+
+        for k in range(group):
+            left, right = pairs[k]
+            for at in range(0, cols, tile):
+                scores = jnp.dot(left[at : at + tile], right, preferred_element_type=F32)
+                total[at : at + tile, :] += jnp.exp2(scores * factor)
         return carry
 
-    lax.fori_loop(0, heads, plain_head, 0)
-    y, core = place[0], place[1]
+    lax.fori_loop(0, heads // group, some_heads, 0)
+    y, core = lax.axis_index("y"), lax.axis_index("core")
     for r in range(NY):
         base = lax.rem(y + r, NY) * (NC * rows)
         mine = pl.multiple_of(base + core * rows, rows)
@@ -73,13 +82,13 @@
         send[r] = total[pl.ds(other, rows), :].astype(BF16)
 
 
-def head_scores(place, queries, keys, logs, rows, scale):
+def head_scores(queries, keys, logs, rows, scale):
     heads, depth, count = queries.shape
     width = keys.shape[2]
     out = jax.ShapeDtypeStruct((NY, rows, width), BF16)
     return pl.pallas_call(
         functools.partial(score_kernel, rows=rows, scale=scale),
-        in_specs=[SCALARS, AWAY, AWAY, HERE],
+        in_specs=[AWAY, AWAY, HERE],
         out_specs=[HERE, HERE],
         scratch_shapes=[
             pltpu.VMEM(queries.shape, BF16),
@@ -95,7 +104,7 @@
             transcendentals=heads * count * width,
         ),
         name="head_scores",
-    )(place, queries, keys, logs)
+    )(queries, keys, logs)
 
 
 def column(array, index):
@@ -200,7 +209,7 @@
         out[at : at + half] = term.astype(BF16).reshape(half, rows, depth)
 
 
-def far_kernel(place, expo, sums, probs, stats, loss, mask, keys, grads, one, two, three):
+def far_kernel(expo, sums, probs, stats, loss, mask, keys, grads, one, two, three):
     rows = expo.shape[0]
     each = stats[...]
     tops = each[:, 0, :]
@@ -215,17 +224,17 @@
     values = (weight * (soft - target)).astype(BF16)
     grads[...] = values
     for r, out in ((1, one), (2, two), (3, three)):
-        first = lax.rem(place[2] + r, NX) * out.shape[0]
+        first = lax.rem(lax.axis_index("x") + r, NX) * out.shape[0]
         query_terms(mask, first, keys, values, out)
 
 
-def far_terms(place, expo, sums, probs, stats, loss, mask, keys):
+def far_terms(expo, sums, probs, stats, loss, mask, keys):
     heads, rows, width = mask.shape
     depth = keys.shape[1]
     part = jax.ShapeDtypeStruct((heads // NX, rows, depth), BF16)
     return pl.pallas_call(
         far_kernel,
-        in_specs=[SCALARS] + [HERE] * 7,
+        in_specs=[HERE] * 7,
         out_specs=[HERE] * 4,
         out_shape=[jax.ShapeDtypeStruct((rows, width), BF16), part, part, part],
         compiler_params=SMALL,
@@ -233,14 +242,33 @@
             flops=heads * rows * depth * width, bytes_accessed=8 * MIB, transcendentals=0
         ),
         name="far_terms",
-    )(place, expo, sums, probs, stats, loss, mask, keys)
-
-
-def near_kernel(place, grads, mask, keys, scaled, own, key_part, total):
+    )(expo, sums, probs, stats, loss, mask, keys)
+
+
+def own_kernel(grads, mask, keys, own):
+    query_terms(mask, lax.axis_index("x") * own.shape[0], keys, grads[...], own)
+
+
+def own_terms(grads, mask, keys):
     heads, rows, width = mask.shape
     depth = keys.shape[1]
+    return pl.pallas_call(
+        own_kernel,
+        in_specs=[HERE] * 3,
+        out_specs=HERE,
+        out_shape=jax.ShapeDtypeStruct((heads // NX, rows, depth), BF16),
+        compiler_params=SMALL,
+        cost_estimate=pl.CostEstimate(
+            flops=heads * rows * depth * width // 2, bytes_accessed=2 * MIB, transcendentals=0
+        ),
+        name="own_terms",
+    )(grads, mask, keys)
+
+
+def key_kernel(grads, mask, scaled, keep, send, total):
+    heads, rows, width = mask.shape
+    depth = scaled.shape[2]
     values = grads[...]
-    query_terms(mask, place[2] * own.shape[0], keys, values, own)
     group = 8
     total[...] = jnp.zeros_like(total)
 
@@ -254,65 +282,104 @@
         return carry
 
     lax.fori_loop(0, heads // group, some_heads, 0)
-    key_part[...] = total[...].astype(BF16)
-
-
-def near_terms(place, grads, mask, keys, scaled):
+    y, core = lax.axis_index("y"), lax.axis_index("core")
+    count = keep.shape[1]
+    for r in range(NY):
+        base = lax.rem(y + r, NY) * (NC * count)
+        mine = pl.multiple_of(base + core * count, count)
+        other = pl.multiple_of(base + (1 - core) * count, count)
+        keep[r] = total[pl.ds(mine, count), :].astype(BF16)
+        send[r] = total[pl.ds(other, count), :].astype(BF16)
+
+
+def key_terms(grads, mask, scaled):
     heads, rows, width = mask.shape
-    depth = keys.shape[1]
-    return pl.pallas_call(
-        near_kernel,
-        in_specs=[SCALARS] + [HERE] * 4,
+    depth = scaled.shape[2]
+    out = jax.ShapeDtypeStruct((NY, depth // (NY * NC), width), BF16)
+    return pl.pallas_call(
+        key_kernel,
+        in_specs=[HERE] * 3,
         out_specs=[HERE] * 2,
+        out_shape=[out, out],
         scratch_shapes=[pltpu.VMEM((depth, width), F32)],
-        out_shape=[
-            jax.ShapeDtypeStruct((heads // NX, rows, depth), BF16),
-            jax.ShapeDtypeStruct((depth, width), BF16),
-        ],
         compiler_params=SMALL,
         cost_estimate=pl.CostEstimate(
-            flops=3 * heads * rows * depth * width, bytes_accessed=10 * MIB, transcendentals=0
-        ),
-        name="near_terms",
-    )(place, grads, mask, keys, scaled)
-
-
-def last_kernel(place, pieces, queries, weights, query_grad, weight_grad):
+            flops=2 * heads * rows * depth * width, bytes_accessed=10 * MIB, transcendentals=0
+        ),
+        name="key_terms",
+    )(grads, mask, scaled)
+
+
+def last_kernel(pieces, queries, weights, query_grad, weight_grad):
     summed = pieces[0].astype(F32)
     for k in range(1, pieces.shape[0]):
         summed += pieces[k].astype(F32)
     mine = pieces.shape[1]
+    first = (lax.axis_index("x") * NZ + lax.axis_index("z")) * mine
     every = weights[...].astype(F32)
     for k in range(mine):
-        dots = jnp.sum(summed[k] * queries[k].astype(F32), axis=1, keepdims=True)
+        own = queries[first + k].astype(F32)
+        dots = jnp.sum(summed[k] * own, axis=1, keepdims=True)
         weight_grad[k : k + 1, :] = jnp.broadcast_to(dots, (dots.shape[0], 128)).T[0:1]
-        query_grad[:, k, :] = (summed[k] * column(every, place[3] * mine + k)).astype(BF16)
-
-
-def last_sums(place, pieces, queries, weights):
+        query_grad[:, k, :] = (summed[k] * column(every, first + k)).astype(BF16)
+
+
+def last_sums(pieces, queries, weights):
     count, mine, rows, depth = pieces.shape
     return pl.pallas_call(
         last_kernel,
-        grid_spec=pltpu.PrefetchScalarGridSpec(
-            num_scalar_prefetch=1,
-            grid=(1,),
-            in_specs=[
-                pl.BlockSpec(pieces.shape, lambda i, p: (0, 0, 0, 0)),
-                pl.BlockSpec((mine, rows, depth), lambda i, p: (p[3], 0, 0)),
-                pl.BlockSpec(weights.shape, lambda i, p: (0, 0)),
-            ],
-            out_specs=[
-                pl.BlockSpec((rows, mine, depth), lambda i, p: (0, 0, 0)),
-                pl.BlockSpec((mine, rows), lambda i, p: (0, 0)),
-            ],
-        ),
+        in_specs=[HERE] * 3,
+        out_specs=[HERE] * 2,
         out_shape=[
             jax.ShapeDtypeStruct((rows, mine, depth), BF16),
             jax.ShapeDtypeStruct((mine, rows), F32),
         ],
         compiler_params=SMALL,
         name="last_sums",
-    )(place, pieces, queries, weights)
+    )(pieces, queries, weights)
+
+
+def sum_kernel(*refs, count):
+    total = refs[0][...].astype(F32)
+    for part in refs[1:count]:
+        total += part[...].astype(F32)
+    refs[-1][...] = total.astype(BF16)
+
+
+def sum_parts(parts, name, after=()):
+    return pl.pallas_call(
+        functools.partial(sum_kernel, count=len(parts)),
+        in_specs=[HERE] * (len(parts) + len(after)),
+        out_specs=HERE,
+        out_shape=jax.ShapeDtypeStruct(parts[0].shape, BF16),
+        compiler_params=SMALL,
+        name=name,
+    )(*parts, *after)
+
+
+def pair_kernel(keep, arrived, *outs):
+    for r, out in enumerate(outs):
+        out[...] = (keep[r].astype(F32) + arrived[r].astype(F32)).astype(BF16)
+
+
+def sum_pair(keep, arrived, name):
+    part = jax.ShapeDtypeStruct(keep.shape[1:], BF16)
+    return pl.pallas_call(
+        pair_kernel,
+        in_specs=[HERE] * 2,
+        out_specs=[HERE] * NY,
+        out_shape=[part] * NY,
+        compiler_params=SMALL,
+        name=name,
+    )(keep, arrived)
+
+
+def sum_over_heads(keep, send, name):
+    with jax.named_scope(name + "_core"):
+        arrived = rotate(send, "core", 1)
+    pairs = sum_pair(keep, arrived, name)
+    with jax.named_scope(name + "_y"):
+        return [pairs[0]] + [rotate(pairs[r], "y", r) for r in (2, 1, 3)]
 
 
 def per_device(
@@ -321,20 +388,14 @@
     rows, heads, depth = index_queries.shape
     width = index_keys.shape[0]
     scale = main_queries.shape[2] ** (-0.5)
-    x, z = lax.axis_index("x"), lax.axis_index("z")
-    place = jnp.stack([lax.axis_index("y"), lax.axis_index("core"), x, x * NZ + z])
-
     keep, send = head_scores(
-        place,
         jnp.transpose(main_queries, (1, 2, 0)),
         jnp.transpose(main_keys, (1, 2, 0)),
         log_sums.T,
         rows,
         scale,
     )
-    arrived = rotate(send, "core", 1)
-    pairs = [(keep[r].astype(F32) + arrived[r].astype(F32)).astype(BF16) for r in range(NY)]
-    parts = [pairs[0]] + [rotate(pairs[r], "y", r) for r in range(1, NY)]
+    parts = sum_over_heads(keep, send, "pair_probs")
 
     turned = jnp.transpose(index_queries, (1, 0, 2))
     expo, sums, mask, scaled = index_logits(turned, index_keys, index_weights)
@@ -342,29 +403,25 @@
     probs, stats = local_stats(sums, parts)
     everywhere = lax.all_to_all(stats, ("x", "z"), split_axis=0, concat_axis=0, tiled=True)
     grads, one, two, three = far_terms(
-        place, expo, sums, probs, everywhere, loss_weights[None], mask, index_keys
+        expo, sums, probs, everywhere, loss_weights[None], mask, index_keys
     )
-    across = [rotate(term, "x", r) for r, term in ((1, one), (2, two), (3, three))]
-    own, key_part = near_terms(place, grads, mask, index_keys, scaled)
-    summed = sum(part.astype(F32) for part in [own] + across).astype(BF16)
-    pieces = lax.all_to_all(
-        summed.reshape(NZ, heads // (NX * NZ), rows, depth),
-        "z",
-        split_axis=0,
-        concat_axis=0,
-        tiled=True,
-    )
-    query_grad, weight_grad = last_sums(place, pieces, turned, index_weights)
-
-    key_pieces = lax.all_to_all(
-        key_part.reshape(NY * NC, depth // (NY * NC), width),
-        ("y", "core"),
-        split_axis=0,
-        concat_axis=0,
-        tiled=True,
-    )
-    key_grad = key_pieces.astype(F32).sum(axis=0).astype(BF16).T
-    return query_grad, weight_grad.T, key_grad
+    with jax.named_scope("x_turns"):
+        across = [rotate(term, "x", r) for r, term in ((2, two), (1, one), (3, three))]
+    key_keep, key_send = key_terms(grads, mask, scaled)
+    key_parts = sum_over_heads(key_keep, key_send, "pair_keys")
+    own = own_terms(grads, mask, index_keys)
+    summed = sum_parts([own] + across, "x_sums", key_parts[:1])
+    with jax.named_scope("z_exchange"):
+        pieces = lax.all_to_all(
+            summed.reshape(NZ, heads // (NX * NZ), rows, depth),
+            "z",
+            split_axis=0,
+            concat_axis=0,
+            tiled=True,
+        )
+    query_grad, weight_grad = last_sums(pieces, turned, index_weights)
+    key_grad = sum_parts(key_parts, "key_sums")
+    return query_grad, weight_grad.T, key_grad.T
 
 
 def solution(mesh):

time: 88.8 us -> 76.4 us (0.86)
  Pallas kernels: 24.9 us -> 20.7 us
  other arithmetic: 3.45 us -> 0 us
  waiting for transfers between devices: 18.4 us -> 15.1 us
  starting transfers between devices: 18.6 us -> 16.7 us
    ppermute x7 -> x11, waiting for transfers between devices: 2.12 us -> 10.9 us  [rotate(): return lax.ppermute(array, axis, [(i, (i + shift) % n) for i in range(n)])]
    all_to_all x1, waiting for transfers between devices: 11 us -> 4.19 us  [per_device(): lax.all_to_all(summed.reshape(NZ, heads // (NX * NZ), rows, depth), 'z',...]
    all_to_all x1 -> x0, starting transfers between devices: 6.02 us -> none  [per_device(): lax.all_to_all(key_part.reshape(NY * NC, depth // (NY * NC), width), ('y'...]
    all_to_all x1 -> x0, waiting for transfers between devices: 5.2 us -> none  [per_device(): lax.all_to_all(key_part.reshape(NY * NC, depth // (NY * NC), width), ('y'...]
    ppermute x7 -> x11, starting transfers between devices: 9.16 us -> 13.3 us  [rotate(): return lax.ppermute(array, axis, [(i, (i + shift) % n) for i in range(n)])]
    pallas_call x1, Pallas kernels: 11.3 us -> 7.76 us  [head_scores(): pl.pallas_call(functools.partial(score_kernel, rows=rows, scale=scale), i...]
    convert_element_type x2 -> x0, other arithmetic: 2.13 us -> none  [the longest x1 1.27 us: per_device(): (keep[r].astype(F32) + arrived[r].astype(F32)).astype(BF16)]
    pallas_call x3 -> x8, Pallas kernels: 8.71 us -> 8.01 us  [the longest x1 2.78 us: key_terms(): pl.pallas_call(key_kernel, in_specs=[HERE] * 3, out_specs=[HERE] * 2, out...]
  transfers between devices with their start and end apart: 9 -> 12, of which waited for: 3 -> 9; matrix products, arithmetic and copies ran while one was open for 2% -> 1% of each run, Pallas kernels for 11% -> 12%
where the time goes in v3:
time: 76.4 us; the launch traced here: 76.1 us
  blocking collectives  21.4 us (28%)
  Pallas kernels  20.7 us (27%)
  starting transfers between devices  16.7 us (22%)
  waiting for transfers between devices  15.1 us (20%)
  local copies, waits for them, and re-layouts  1.45 us (2%)
    all_to_all x1, blocking collectives, per_device(): lax.all_to_all(stats, ('x', 'z'), split_axis=0, concat_axis=0, tiled=True)  21.4 us
    ppermute x11, starting transfers between devices, rotate(): return lax.ppermute(array, axis, [(i, (i + shift) % n) for i in range(n)])  13.3 us
    ppermute x11, waiting for transfers between devices, rotate(): return lax.ppermute(array, axis, [(i, (i + shift) % n) for i in range(n)])  10.9 us
    pallas_call x1, Pallas kernels, head_scores(): pl.pallas_call(functools.partial(score_kernel, rows=rows, scale=scale), i...  7.76 us
    pallas_call x1, Pallas kernels, index_logits(): pl.pallas_call(logit_kernel, in_specs=[HERE] * 3, out_specs=[HERE] * 4, o...  4.71 us
    all_to_all x1, waiting for transfers between devices, per_device(): lax.all_to_all(summed.reshape(NZ, heads // (NX * NZ), rows, depth), 'z',...  4.19 us
    all_to_all x1, starting transfers between devices, per_device(): lax.all_to_all(summed.reshape(NZ, heads // (NX * NZ), rows, depth), 'z',...  3.41 us
    pallas_call x1, Pallas kernels, key_terms(): pl.pallas_call(key_kernel, in_specs=[HERE] * 3, out_specs=[HERE] * 2, out...  2.78 us
  transfers between devices with their start and end apart: 12, of which 9 were waited for; matrix products, arithmetic and copies ran while one was open for 1% of the time, Pallas kernels for 12%

profile of v3, /device:TPU:8, one launch (start us, length us, event | category | flops | bytes accessed | tf_op | source)
XLA Modules:
  0.0 76.1 jit_solution(13526081340220797325)
XLA Ops:
  0.6 0.0 copy-start.3
  0.6 0.7 copy-done.3
  1.4 0.0 copy-start.4
  1.4 0.0 copy-start
  1.4 0.0 copy-start.1
  1.4 7.8 %head_scores.1 = (bf16[4,64,1024]{2,1,0:T(8,128)(2,1)S(1)}, bf16[4,64,1024]{2,1,0:T(8,128)(2,1)S(1)}) custom-call(bf16[16,192,512]{2,1,0:T(8,128)(2,1)} %bitcast.16, bf16[16,192,1024]{2,1,0:T(8,128)(2,1)} %bitcast.15, f32[16,512]{1,0:T(8,128)S(1)} %bitcast.13), custom_call_target="tpu_custom_call" | custom-call | flops 3221225472 | bytes 12582912 | tf_op jit(solution)/shard_map/head_scores/pallas_call | solution.py:89
  9.2 0.0 copy-start.2
  9.2 0.1 collective-permute-start
  9.3 1.9 %collective-permute-done.arrived = bf16[4,64,1024]{2,1,0:T(8,128)(2,1)S(1)} collective-permute-done((bf16[4,64,1024]{2,1,0:T(8,128)(2,1)S(1)}, bf16[4,64,1024]{2,1,0:T(8,128)(2,1)S(1)}, u32[]{:S(2)}, u32[]{:S(2)}) %collective-permute-start) | collective-permute-done | bytes 524320 | tf_op jit(solution)/shard_map/pair_probs_core/ppermute | solution.py:23
  11.2 0.1 pair_probs.1
  11.3 2.4 %collective-permute-start.1 = (bf16[64,1024]{1,0:T(8,128)(2,1)S(1)}, bf16[64,1024]{1,0:T(8,128)(2,1)S(1)}, u32[]{:S(2)}, u32[]{:S(2)}) collective-permute-start(bf16[64,1024]{1,0:T(8,128)(2,1)S(1)} %get-tuple-element.32), channel_id=1, source_target_pairs={{0,128},{64,192},{128,0},{192,64},{1,129},{65,193},{129,1},{193,65... | collective-permute-start | bytes 393224 | tf_op jit(solution)/shard_map/pair_probs_y/ppermute | solution.py:23
  13.7 1.3 %collective-permute-start.2 = (bf16[64,1024]{1,0:T(8,128)(2,1)S(1)}, bf16[64,1024]{1,0:T(8,128)(2,1)S(1)}, u32[]{:S(2)}, u32[]{:S(2)}) collective-permute-start(bf16[64,1024]{1,0:T(8,128)(2,1)S(1)} %get-tuple-element.33), channel_id=1, source_target_pairs={{0,64},{64,128},{128,192},{192,0},{1,65},{65,129},{129,193},{193,1... | collective-permute-start | bytes 393224 | tf_op jit(solution)/shard_map/pair_probs_y/ppermute | solution.py:23
  15.0 0.7 collective-permute-start.3
  15.7 0.0 copy-done.4
  15.7 0.7 copy.12
  16.4 0.0 copy-done
  16.4 0.0 copy-done.1
  16.4 4.7 %index_logits.1 = (f32[64,1024]{1,0:T(8,128)S(1)}, f32[64,128]{1,0:T(8,128)S(1)}, bf16[64,64,1024]{2,1,0:T(8,128)(2,1)S(1)}, bf16[64,64,128]{2,1,0:T(8,128)(2,1)S(1)}) custom-call(bf16[64,64,128]{2,1,0:T(8,128)(2,1)S(1)} %bitcast.10, bf16[1024,128]{1,0:T(8,128)(2,1)S(1)} %copy-done, bf16[64,64]{1,0:T(8,128)(2,1)S(1)} %copy-done.1), custom_call_target="tpu_custom_call" | custom-call | flops 1073741824 | bytes 10485760 | tf_op jit(solution)/shard_map/index_logits/pallas_call | solution.py:153
  21.1 0.0 collective-permute-done.1.two
  21.1 0.2 collective-permute-done.2.three
  21.4 0.0 collective-permute-done.3.four
  21.4 0.2 local_stats.1
  21.6 21.4 %all_to_all.10.stats = f32[32,8,128]{2,1,0:T(8,128)S(1)} all-to-all(f32[32,8,128]{2,1,0:T(8,128)S(1)} %get-tuple-element.36), channel_id=1, replica_groups=mesh['y'=4,'core'=2,'x'=4,'z'=8] {'x','z'}, dimensions={0} | all-to-all | bytes 262144 | tf_op jit(solution)/shard_map/all_to_all | solution.py:404
  43.0 0.0 copy-done.2
  43.0 2.1 %far_terms.1 = (bf16[64,1024]{1,0:T(8,128)(2,1)S(1)}, bf16[16,64,128]{2,1,0:T(8,128)(2,1)S(1)}, bf16[16,64,128]{2,1,0:T(8,128)(2,1)S(1)}, bf16[16,64,128]{2,1,0:T(8,128)(2,1)S(1)}) custom-call(f32[64,1024]{1,0:T(8,128)S(1)} %get-tuple-element.27.expo, f32[64,128]{1,0:T(8,128)S(1)} %get-tuple-element.28.sums, f32[64,1024]{1,0:T(8,128)S(1)} %get-tuple-element.35.probs, ...), custom_call_target="tpu_custom_call" | custom-call | flops 536870912 | bytes 8388608 | tf_op jit(solution)/shard_map/far_terms/pallas_call | solution.py:235
  45.1 1.5 %collective-permute-start.4 = (bf16[16,64,128]{2,1,0:T(8,128)(2,1)S(1)}, bf16[16,64,128]{2,1,0:T(8,128)(2,1)S(1)}, u32[]{:S(2)}, u32[]{:S(2)}) collective-permute-start(bf16[16,64,128]{2,1,0:T(8,128)(2,1)S(1)} %get-tuple-element.39), channel_id=1, source_target_pairs={{0,16},{8,24},{16,0},{24,8},{1,17},{9,25},{17,1},{25,9},{2,18},{10... | collective-permute-start | bytes 786440 | tf_op jit(solution)/shard_map/x_turns/ppermute | solution.py:23
  46.6 0.6 collective-permute-start.5
  47.2 2.7 %collective-permute-start.6 = (bf16[16,64,128]{2,1,0:T(8,128)(2,1)S(1)}, bf16[16,64,128]{2,1,0:T(8,128)(2,1)S(1)}, u32[]{:S(2)}, u32[]{:S(2)}) collective-permute-start(bf16[16,64,128]{2,1,0:T(8,128)(2,1)S(1)} %get-tuple-element.41), channel_id=1, source_target_pairs={{0,24},{8,0},{16,8},{24,16},{1,25},{9,1},{17,9},{25,17},{2,26},{10... | collective-permute-start | bytes 786440 | tf_op jit(solution)/shard_map/x_turns/ppermute | solution.py:23
  49.9 2.8 %key_terms.1 = (bf16[4,16,1024]{2,1,0:T(8,128)(2,1)S(1)}, bf16[4,16,1024]{2,1,0:T(8,128)(2,1)S(1)}) custom-call(bf16[64,1024]{1,0:T(8,128)(2,1)S(1)} %get-tuple-element.38.grads, bf16[64,64,1024]{2,1,0:T(8,128)(2,1)S(1)} %get-tuple-element.37.mask, bf16[64,64,128]{2,1,0:T(8,128)(2,1)S(1)} %get-tuple-element.42.scaled), custom_call_target="tpu_custom_call" | custom-call | flops 1073741824 | bytes 10485760 | tf_op jit(solution)/shard_map/key_terms/pallas_call | solution.py:299
  52.6 0.1 collective-permute-start.7
  52.7 0.7 own_terms.1.refs_0_
  53.5 0.6 collective-permute-done.7.arrived
  54.1 1.8 %collective-permute-done.4.refs_1_ = bf16[16,64,128]{2,1,0:T(8,128)(2,1)S(1)} collective-permute-done((bf16[16,64,128]{2,1,0:T(8,128)(2,1)S(1)}, bf16[16,64,128]{2,1,0:T(8,128)(2,1)S(1)}, u32[]{:S(2)}, u32[]{:S(2)}) %collective-permute-start.4) | collective-permute-done | bytes 262176 | tf_op jit(solution)/shard_map/x_turns/ppermute | solution.py:23
  55.9 3.1 %collective-permute-done.5.refs_2_ = bf16[16,64,128]{2,1,0:T(8,128)(2,1)S(1)} collective-permute-done((bf16[16,64,128]{2,1,0:T(8,128)(2,1)S(1)}, bf16[16,64,128]{2,1,0:T(8,128)(2,1)S(1)}, u32[]{:S(2)}, u32[]{:S(2)}) %collective-permute-start.5) | collective-permute-done | bytes 262176 | tf_op jit(solution)/shard_map/x_turns/ppermute | solution.py:23
  59.0 0.0 collective-permute-done.6.refs_3_
  59.0 0.8 %x_sums.1 = bf16[16,64,128]{2,1,0:T(8,128)(2,1)} custom-call(bf16[16,64,128]{2,1,0:T(8,128)(2,1)S(1)} %own_terms.1.refs_0_, bf16[16,64,128]{2,1,0:T(8,128)(2,1)S(1)} %collective-permute-done.4.refs_1_, bf16[16,64,128]{2,1,0:T(8,128)(2,1)S(1)} %collective-permute-done.5.refs_2_, bf16[16,64,128]{2,1,0:T(8,128)(2,1)S(1)} %collective-permute-done.6.refs_3_, ...), custom_call_target="tpu_custom_call" | custom-call | tf_op jit(solution)/shard_map/x_sums/pallas_call | solution.py:350
  59.8 3.4 %all-to-all-start.1 = ((bf16[8,2,64,128]{3,2,1,0:T(8,128)(2,1)}), bf16[8,2,64,128]{3,2,1,0:T(8,128)(2,1)S(1)}, u32[]{:S(2)}, u32[]{:S(2)}) async-start(bf16[8,2,64,128]{3,2,1,0:T(8,128)(2,1)} %bitcast.5), calls=%async_computation.1 | async-start | bytes 524288 | tf_op jit(solution)/shard_map/z_exchange/all_to_all | solution.py:415
  63.2 1.9 %collective-permute-start.8 = (bf16[16,1024]{1,0:T(8,128)(2,1)S(1)}, bf16[16,1024]{1,0:T(8,128)(2,1)S(1)}, u32[]{:S(2)}, u32[]{:S(2)}) collective-permute-start(bf16[16,1024]{1,0:T(8,128)(2,1)S(1)} %get-tuple-element.48), channel_id=1, source_target_pairs={{0,128},{64,192},{128,0},{192,64},{1,129},{65,193},{129,1},{193,65... | collective-permute-start | bytes 98312 | tf_op jit(solution)/shard_map/pair_keys_y/ppermute | solution.py:23
  65.1 1.4 %collective-permute-start.9 = (bf16[16,1024]{1,0:T(8,128)(2,1)S(1)}, bf16[16,1024]{1,0:T(8,128)(2,1)S(1)}, u32[]{:S(2)}, u32[]{:S(2)}) collective-permute-start(bf16[16,1024]{1,0:T(8,128)(2,1)S(1)} %get-tuple-element.49), channel_id=1, source_target_pairs={{0,64},{64,128},{128,192},{192,0},{1,65},{65,129},{129,193},{193,1... | collective-permute-start | bytes 98312 | tf_op jit(solution)/shard_map/pair_keys_y/ppermute | solution.py:23
  66.5 0.6 collective-permute-start.10
  67.2 1.6 %collective-permute-done.8.refs_1_ = bf16[16,1024]{1,0:T(8,128)(2,1)S(1)} collective-permute-done((bf16[16,1024]{1,0:T(8,128)(2,1)S(1)}, bf16[16,1024]{1,0:T(8,128)(2,1)S(1)}, u32[]{:S(2)}, u32[]{:S(2)}) %collective-permute-start.8) | collective-permute-done | bytes 32800 | tf_op jit(solution)/shard_map/pair_keys_y/ppermute | solution.py:23
  68.8 0.3 collective-permute-done.9.refs_2_
  69.0 1.4 %collective-permute-done.10.refs_3_ = bf16[16,1024]{1,0:T(8,128)(2,1)S(1)} collective-permute-done((bf16[16,1024]{1,0:T(8,128)(2,1)S(1)}, bf16[16,1024]{1,0:T(8,128)(2,1)S(1)}, u32[]{:S(2)}, u32[]{:S(2)}) %collective-permute-start.10) | collective-permute-done | bytes 32800 | tf_op jit(solution)/shard_map/pair_keys_y/ppermute | solution.py:23
  70.4 0.6 key_sums.1
  71.1 4.2 %all-to-all-done.1.pieces = bf16[8,2,64,128]{3,2,1,0:T(8,128)(2,1)S(1)} async-done(((bf16[8,2,64,128]{3,2,1,0:T(8,128)(2,1)}), bf16[8,2,64,128]{3,2,1,0:T(8,128)(2,1)S(1)}, u32[]{:S(2)}, u32[]{:S(2)}) %all-to-all-start.1) | async-done | bytes 262176 | tf_op jit(solution)/shard_map/z_exchange/all_to_all | solution.py:415
  75.3 0.8 %last_sums.1 = (bf16[64,2,128]{2,1,0:T(2,128)(2,1)}, f32[2,64]{1,0:T(2,128)}) custom-call(bf16[8,2,64,128]{3,2,1,0:T(8,128)(2,1)S(1)} %all-to-all-done.1.pieces, bf16[64,64,128]{2,1,0:T(8,128)(2,1)S(1)} %bitcast.11, bf16[64,64]{1,0:T(8,128)(2,1)S(1)} %copy-done.1), custom_call_target="tpu_custom_call" | custom-call | tf_op jit(solution)/shard_map/last_sums/pallas_call | solution.py:329
  (1 shorter events, 0.0 us)
Async XLA Ops:
  0.6 0.8 copy-start.3
  1.4 14.3 %copy-start.4 = (bf16[64,64,128]{2,1,0:T(8,128)(2,1)S(1)}, bf16[64,64,128]{2,1,0:T(8,128)(2,1)}, u32[]{:S(2)}) copy-start(bf16[64,64,128]{2,1,0:T(8,128)(2,1)} %param.10) | copy-start | bytes 3145732
  1.4 15.0 %copy-start = (bf16[1024,128]{1,0:T(8,128)(2,1)S(1)}, bf16[1024,128]{1,0:T(8,128)(2,1)}, u32[]{:S(2)}) copy-start(bf16[1024,128]{1,0:T(8,128)(2,1)} %keys.5) | copy-start | bytes 786436
  1.4 15.0 %copy-start.1 = (bf16[64,64]{1,0:T(8,128)(2,1)S(1)}, bf16[64,64]{1,0:T(8,128)(2,1)}, u32[]{:S(2)}) copy-start(bf16[64,64]{1,0:T(8,128)(2,1)} %weights.3) | copy-start | bytes 24580
  9.2 33.8 %copy-start.2 = (f32[64]{0:T(128)S(1)}, f32[64]{0:T(128)}, u32[]{:S(2)}) copy-start(f32[64]{0:T(128)} %param.13) | copy-start | bytes 772
  9.2 2.0 %collective-permute-start = (bf16[4,64,1024]{2,1,0:T(8,128)(2,1)S(1)}, bf16[4,64,1024]{2,1,0:T(8,128)(2,1)S(1)}, u32[]{:S(2)}, u32[]{:S(2)}) collective-permute-start(bf16[4,64,1024]{2,1,0:T(8,128)(2,1)S(1)} %get-tuple-element.30), channel_id=1, source_target_pairs={{0,32},{32,0},{1,33},{33,1},{2,34},{34,2},{3,35},{35,3},{4,36},{36... | collective-permute-start | bytes 1572872 | tf_op jit(solution)/shard_map/pair_probs_core/ppermute | solution.py:23
  11.3 9.8 %collective-permute-start.1 = (bf16[64,1024]{1,0:T(8,128)(2,1)S(1)}, bf16[64,1024]{1,0:T(8,128)(2,1)S(1)}, u32[]{:S(2)}, u32[]{:S(2)}) collective-permute-start(bf16[64,1024]{1,0:T(8,128)(2,1)S(1)} %get-tuple-element.32), channel_id=1, source_target_pairs={{0,128},{64,192},{128,0},{192,64},{1,129},{65,193},{129,1},{193,65... | collective-permute-start | bytes 393224 | tf_op jit(solution)/shard_map/pair_probs_y/ppermute | solution.py:23
  13.7 7.7 %collective-permute-start.2 = (bf16[64,1024]{1,0:T(8,128)(2,1)S(1)}, bf16[64,1024]{1,0:T(8,128)(2,1)S(1)}, u32[]{:S(2)}, u32[]{:S(2)}) collective-permute-start(bf16[64,1024]{1,0:T(8,128)(2,1)S(1)} %get-tuple-element.33), channel_id=1, source_target_pairs={{0,64},{64,128},{128,192},{192,0},{1,65},{65,129},{129,193},{193,1... | collective-permute-start | bytes 393224 | tf_op jit(solution)/shard_map/pair_probs_y/ppermute | solution.py:23
  15.0 6.4 %collective-permute-start.3 = (bf16[64,1024]{1,0:T(8,128)(2,1)S(1)}, bf16[64,1024]{1,0:T(8,128)(2,1)S(1)}, u32[]{:S(2)}, u32[]{:S(2)}) collective-permute-start(bf16[64,1024]{1,0:T(8,128)(2,1)S(1)} %get-tuple-element.34), channel_id=1, source_target_pairs={{0,192},{64,0},{128,64},{192,128},{1,193},{65,1},{129,65},{193,129... | collective-permute-start | bytes 393224 | tf_op jit(solution)/shard_map/pair_probs_y/ppermute | solution.py:23
  45.1 10.8 %collective-permute-start.4 = (bf16[16,64,128]{2,1,0:T(8,128)(2,1)S(1)}, bf16[16,64,128]{2,1,0:T(8,128)(2,1)S(1)}, u32[]{:S(2)}, u32[]{:S(2)}) collective-permute-start(bf16[16,64,128]{2,1,0:T(8,128)(2,1)S(1)} %get-tuple-element.39), channel_id=1, source_target_pairs={{0,16},{8,24},{16,0},{24,8},{1,17},{9,25},{17,1},{25,9},{2,18},{10... | collective-permute-start | bytes 786440 | tf_op jit(solution)/shard_map/x_turns/ppermute | solution.py:23
  46.6 12.3 %collective-permute-start.5 = (bf16[16,64,128]{2,1,0:T(8,128)(2,1)S(1)}, bf16[16,64,128]{2,1,0:T(8,128)(2,1)S(1)}, u32[]{:S(2)}, u32[]{:S(2)}) collective-permute-start(bf16[16,64,128]{2,1,0:T(8,128)(2,1)S(1)} %get-tuple-element.40), channel_id=1, source_target_pairs={{0,8},{8,16},{16,24},{24,0},{1,9},{9,17},{17,25},{25,1},{2,10},{10... | collective-permute-start | bytes 786440 | tf_op jit(solution)/shard_map/x_turns/ppermute | solution.py:23
  47.2 11.8 %collective-permute-start.6 = (bf16[16,64,128]{2,1,0:T(8,128)(2,1)S(1)}, bf16[16,64,128]{2,1,0:T(8,128)(2,1)S(1)}, u32[]{:S(2)}, u32[]{:S(2)}) collective-permute-start(bf16[16,64,128]{2,1,0:T(8,128)(2,1)S(1)} %get-tuple-element.41), channel_id=1, source_target_pairs={{0,24},{8,0},{16,8},{24,16},{1,25},{9,1},{17,9},{25,17},{2,26},{10... | collective-permute-start | bytes 786440 | tf_op jit(solution)/shard_map/x_turns/ppermute | solution.py:23
  52.6 1.4 %collective-permute-start.7 = (bf16[4,16,1024]{2,1,0:T(8,128)(2,1)S(1)}, bf16[4,16,1024]{2,1,0:T(8,128)(2,1)S(1)}, u32[]{:S(2)}, u32[]{:S(2)}) collective-permute-start(bf16[4,16,1024]{2,1,0:T(8,128)(2,1)S(1)} %get-tuple-element.44), channel_id=1, source_target_pairs={{0,32},{32,0},{1,33},{33,1},{2,34},{34,2},{3,35},{35,3},{4,36},{36... | collective-permute-start | bytes 393224 | tf_op jit(solution)/shard_map/pair_keys_core/ppermute | solution.py:23
  59.8 15.5 %all-to-all-start.1 = ((bf16[8,2,64,128]{3,2,1,0:T(8,128)(2,1)}), bf16[8,2,64,128]{3,2,1,0:T(8,128)(2,1)S(1)}, u32[]{:S(2)}, u32[]{:S(2)}) async-start(bf16[8,2,64,128]{3,2,1,0:T(8,128)(2,1)} %bitcast.5), calls=%async_computation.1 | async-start | bytes 524288 | tf_op jit(solution)/shard_map/z_exchange/all_to_all | solution.py:415
  63.2 5.5 %collective-permute-start.8 = (bf16[16,1024]{1,0:T(8,128)(2,1)S(1)}, bf16[16,1024]{1,0:T(8,128)(2,1)S(1)}, u32[]{:S(2)}, u32[]{:S(2)}) collective-permute-start(bf16[16,1024]{1,0:T(8,128)(2,1)S(1)} %get-tuple-element.48), channel_id=1, source_target_pairs={{0,128},{64,192},{128,0},{192,64},{1,129},{65,193},{129,1},{193,65... | collective-permute-start | bytes 98312 | tf_op jit(solution)/shard_map/pair_keys_y/ppermute | solution.py:23
  65.1 3.9 %collective-permute-start.9 = (bf16[16,1024]{1,0:T(8,128)(2,1)S(1)}, bf16[16,1024]{1,0:T(8,128)(2,1)S(1)}, u32[]{:S(2)}, u32[]{:S(2)}) collective-permute-start(bf16[16,1024]{1,0:T(8,128)(2,1)S(1)} %get-tuple-element.49), channel_id=1, source_target_pairs={{0,64},{64,128},{128,192},{192,0},{1,65},{65,129},{129,193},{193,1... | collective-permute-start | bytes 98312 | tf_op jit(solution)/shard_map/pair_keys_y/ppermute | solution.py:23
  66.5 3.9 %collective-permute-start.10 = (bf16[16,1024]{1,0:T(8,128)(2,1)S(1)}, bf16[16,1024]{1,0:T(8,128)(2,1)S(1)}, u32[]{:S(2)}, u32[]{:S(2)}) collective-permute-start(bf16[16,1024]{1,0:T(8,128)(2,1)S(1)} %get-tuple-element.50), channel_id=1, source_target_pairs={{0,192},{64,0},{128,64},{192,128},{1,193},{65,1},{129,65},{193,129... | collective-permute-start | bytes 98312 | tf_op jit(solution)/shard_map/pair_keys_y/ppermute | solution.py:23
